TPU v7x, 32 devices: a whole 2x2x4 slice. The times are simulated.
32 devices in a mesh: dp: 8 (over y, x, core), seq: 4 (over z).
Axes of the slice: x: 2, y: 2, z: 4, core: 2. Of those that a mesh axis runs over, the one named last changes fastest.
Arguments:
- tokens: int32 [8, 1024], P('dp', 'seq'), may hold values from 0 to 3
- embedding: float32 [4, 384], replicated, may hold values from -6 to 6
- gain_in: float32 [384], replicated, may hold values from 0.5 to 1.5
- conv_taps: float32 [384, 4], replicated, may hold values from -3 to 3
- long_filter: float32 [384, 1024], P('seq'), may hold values from -6 to 6
- gain_mid: float32 [384], replicated, may hold values from 0.5 to 1.5
- mlp_weights: bfloat16 [2304, 384], replicated, may hold values from -0.3125 to 0.3125
- cotangent: bfloat16 [8, 768, 1024], P('dp', None, 'seq'), may hold values from -6 to 6
Outputs:
- layer_out: bfloat16 [8, 768, 1024], P('dp', None, 'seq')
- grad_embedding: float32 [4, 384], replicated
- grad_gain_in: float32 [384], replicated
- grad_conv: float32 [384, 4], replicated
- grad_filter: float32 [384, 1024], P('seq')
- grad_gain_mid: float32 [384], replicated
- grad_mlp: float32 [2304, 384], P('dp', 'seq')
All inputs are finite; a program needn't handle non-finite values.
Results may differ from a plain program's by a relative error of at most 0.03.
Values may be sent and summed in bfloat16 or wider, within the bound.
A program may use at most 64 MiB of HBM per device.

v0:
```python
import jax
import jax.numpy as jnp
import numpy as np
from jax import lax
from jax.experimental import pallas as pl
from jax.experimental.pallas import tpu as pltpu
from jax.sharding import PartitionSpec as P

F32 = jnp.float32
BF16 = jnp.bfloat16


def dct_table(length):
    freq = np.arange(length)[:, None]
    place = np.arange(length)[None, :]
    phase = (2 * place + 1) * freq % (4 * length)
    weight = np.where(freq == 0, np.sqrt(1.0 / length), np.sqrt(2.0 / length))
    return (weight * np.cos(np.pi * phase / (2 * length))).astype(np.float32).astype(BF16)


def dot(a, b, dims):
    return lax.dot_general(a, b, (dims, ((), ())), preferred_element_type=F32)


def local_kernel(
    n_seq, n_dp, tidy, all_ids, ids, table, packed, filt, mlp, cot,
    out, mlp_a, mlp_b, filt_out, small, full, spec_ref, level_ref, normed_ref, d_normed_ref, down_ref,
):
    channels, block_len = filt.shape[0] * filt.shape[1], filt.shape[2]
    local_len = ids.shape[1]
    hidden = mlp.shape[0] // 3
    n_taps = packed.shape[1] - 6
    emb_cols, gain_in, gain_mid = packed[:, :4], packed[:, 4:5], packed[:, 5:6]
    taps = packed[:, 6:]
    half = 4 * n_taps
    cut = mlp_a.shape[1]
    place = lax.axis_index("seq")
    per_block = block_len // local_len
    first = place // per_block * per_block
    last = first + per_block - 1
    offset = pl.multiple_of((place - first) * local_len, local_len)
    emb = emb_cols
    base_scale = lax.rsqrt(jnp.mean(emb * emb, axis=0, keepdims=True) + 1e-6)
    base_norm = (emb * base_scale * gain_in).astype(BF16).astype(F32)
    lane = lax.broadcasted_iota(jnp.int32, (channels, half), 1)
    tap_part = jnp.zeros((channels, half), F32)
    base_part = jnp.zeros((channels, half), F32)
    for k in range(n_taps):
        tap_part = jnp.where(lane // 4 == k, taps[:, k : k + 1], tap_part)
    for a in range(4):
        base_part = jnp.where(lane % 4 == a, base_norm[:, a : a + 1], base_part)
    kmer = (tap_part * base_part).astype(BF16)
    edge = 128
    before = jnp.where(first > 0, all_ids[jnp.maximum(first - 1, 0)][:, local_len - edge :], 4)
    after = jnp.where(last < n_seq - 1, all_ids[jnp.minimum(last + 1, n_seq - 1)][:, :edge], 4)
    row = jnp.concatenate([before] + [all_ids[first + j] for j in range(per_block)] + [after], 1)
    width = block_len + 2 * edge
    wide = jnp.broadcast_to(row, (8, width))
    sub = lax.broadcasted_iota(jnp.int32, (8, block_len), 0)
    tiles = []
    for s in range(2):
        for k in range(0, n_taps, 2):
            shifts = [(k + i) if s == 0 else (width - k - i) % width for i in range(2)]
            moved = [(pltpu.roll(wide, sh, 1) if sh else wide)[:, edge : edge + block_len] for sh in shifts]
            picked = jnp.where(sub < 4, moved[0], moved[1])
            want = sub % 4 if s == 0 else 3 - sub % 4
            tiles.append(jnp.where(picked == want, 1.0, 0.0))
    hot = jnp.concatenate(tiles, 0).astype(BF16)
    hot_spec = dot(hot, table[...], ((1,), (0,))).astype(BF16)
    rows = filt.shape[1]
    for j in range(n_seq):
        full[j * rows : (j + 1) * rows, :] = filt[j].astype(F32)
    own = ids[...]
    emb_all = emb_cols
    q_own = table[pl.ds(offset, local_len), :]
    for s in range(2):
        spec = dot(kmer, hot_spec[s * half : (s + 1) * half], ((1,), (0,))).astype(BF16)
        spec_ref[s] = spec
        scaled = (full[...] * spec.astype(F32)).astype(BF16)
        mine = own if s == 0 else 3 - own
        level = dot(scaled, q_own, ((1,), (1,)))
        residual = jnp.zeros((channels, local_len), F32)
        for a in range(4):
            residual = jnp.where(mine == a, emb_all[:, a : a + 1], residual)
        level_ref[:, s * local_len : (s + 1) * local_len] = level + residual
    level = level_ref[...]
    mid_scale = lax.rsqrt(jnp.mean(level * level, axis=0, keepdims=True) + 1e-6)
    normed_ref[...] = (level * mid_scale * gain_mid).astype(BF16)
    turn = jnp.where(
        lax.broadcasted_iota(jnp.int32, (channels, channels), 0)
        + lax.broadcasted_iota(jnp.int32, (channels, channels), 1)
        == channels - 1,
        1.0,
        0.0,
    ).astype(BF16)
    turned = dot(turn, cot[channels:, :], ((1,), (0,))).astype(BF16)
    back = jnp.concatenate([cot[:channels, :], turned], 1)
    normed = normed_ref[...]
    tile = 256 if hidden % 256 == 0 else hidden
    for t in range(hidden // tile):
        g0, u0, w0 = t * tile, hidden + t * tile, 2 * hidden + t * tile
        w_gate, w_up, w_down = mlp[g0 : g0 + tile, :], mlp[u0 : u0 + tile, :], mlp[w0 : w0 + tile, :]
        gate = dot(w_gate, normed, ((1,), (0,)))
        up = dot(w_up, normed, ((1,), (0,)))
        d_act = dot(w_down, back, ((1,), (0,)))
        sig = jax.nn.sigmoid(gate)
        silu = gate * sig
        act = (silu * up).astype(BF16)
        d_gate = (d_act * up * (sig + silu * (1.0 - sig))).astype(BF16)
        d_up = (d_act * silu).astype(BF16)
        down = dot(w_down, act, ((0,), (0,)))
        down_ref[...] = down if t == 0 else down_ref[...] + down
        d_part = dot(w_gate, d_gate, ((0,), (0,))) + dot(w_up, d_up, ((0,), (0,)))
        d_normed_ref[...] = d_part if t == 0 else d_normed_ref[...] + d_part
        for start, left, right in ((g0, d_gate, normed), (u0, d_up, normed), (w0, act, back)):
            grad = dot(left, right, ((1,), (1,))).astype(BF16)
            mlp_a[start : start + tile, :] = grad[:, :cut]
            mlp_b[start : start + tile, :] = grad[:, cut:]
    combined = (level_ref[...] + down_ref[...]).astype(BF16)
    out[:channels, :] = combined[:, :local_len]
    out[channels:, :] = dot(turn, combined[:, local_len:], ((1,), (0,))).astype(BF16)
    unit = level * mid_scale
    d_normed = d_normed_ref[...]
    mid_grad = d_normed * unit
    d_unit = d_normed * gain_mid
    d_level = back.astype(F32) + mid_scale * (d_unit - unit * jnp.mean(d_unit * unit, axis=0, keepdims=True))
    d_bf = d_level.astype(BF16)
    d_low = (d_level - d_bf.astype(F32)).astype(BF16)
    both = jnp.concatenate([own, 3 - own], 1)
    sub8 = lax.broadcasted_iota(jnp.int32, (8, 2 * local_len), 0)
    own_hot = jnp.where(sub8 == both, 1.0, 0.0).astype(BF16)
    ones = jnp.ones((8, 2 * local_len), BF16)
    m_bf = mid_grad.astype(BF16)
    m_low = (mid_grad - m_bf.astype(F32)).astype(BF16)
    small[half : half + 8, :] = dot(own_hot, d_bf, ((1,), (1,))) + dot(own_hot, d_low, ((1,), (1,)))
    small[half + 8 : half + 16, :] = dot(ones, m_bf, ((1,), (1,))) + dot(ones, m_low, ((1,), (1,)))
    q_rows = table[pl.ds(offset, local_len), :]
    grad_filter = jnp.zeros((channels, block_len), F32)
    kmer_sum = jnp.zeros((half, channels), F32)
    for s in range(2):
        d_scaled = dot(d_bf[:, s * local_len : (s + 1) * local_len], q_rows, ((1,), (0,)))
        grad_filter = grad_filter + d_scaled * spec_ref[s].astype(F32)
        d_spec = (full[...] * d_scaled).astype(BF16)
        kmer_sum = kmer_sum + dot(hot_spec[s * half : (s + 1) * half], d_spec, ((1,), (1,)))
    small[:half, :] = kmer_sum
    grad_filter = grad_filter.astype(BF16)
    if tidy:
        piece = block_len // n_dp
        for i in range(n_dp):
            filt_out[i] = grad_filter[:, i * piece : (i + 1) * piece]
    else:
        filt_out[...] = grad_filter


def compute(n_seq, n_dp, all_ids, ids, embedding, gain_in, conv_taps, filt, gain_mid, mlp, cot):
    channels = embedding.shape[1]
    block_len = filt.shape[-1]
    local_len = ids.shape[1]
    table = jnp.asarray(dct_table(block_len).T)
    cut = channels // 128 * 2 // 3 * 128
    tidy = block_len % (n_dp * 128) == 0
    f_shape = (n_dp, channels, block_len // n_dp) if tidy else (channels, block_len)
    sums = 4 * conv_taps.shape[1] + 16
    packed = jnp.concatenate([embedding, gain_in[None, :], gain_mid[None, :], conv_taps.T], 0).T
    vmem = pl.BlockSpec(memory_space=pltpu.VMEM)
    return pl.pallas_call(
        lambda *refs: local_kernel(n_seq, n_dp, tidy, *refs),
        out_shape=(
            jax.ShapeDtypeStruct(cot.shape, BF16),
            jax.ShapeDtypeStruct((mlp.shape[0], cut), BF16),
            jax.ShapeDtypeStruct((mlp.shape[0], channels - cut), BF16),
            jax.ShapeDtypeStruct(f_shape, BF16),
            jax.ShapeDtypeStruct((sums, channels), F32),
        ),
        in_specs=[vmem] * 7,
        out_specs=[vmem] * 5,
        scratch_shapes=[
            pltpu.VMEM((channels, block_len), F32),
            pltpu.VMEM((2, channels, block_len), BF16),
            pltpu.VMEM((channels, 2 * local_len), F32),
            pltpu.VMEM((channels, 2 * local_len), BF16),
            pltpu.VMEM((channels, 2 * local_len), F32),
            pltpu.VMEM((channels, 2 * local_len), F32),
        ],
        compiler_params=pltpu.CompilerParams(vmem_limit_bytes=36 * 2**20),
        name="local",
    )(all_ids, ids, table, packed, filt, mlp, cot)


def finish_kernel(small, embedding, gain_in, taps, grad_emb, grad_gain, grad_conv, grad_mid):
    n_taps = taps.shape[0]
    emb = embedding[...]
    base_scale = lax.rsqrt(jnp.mean(emb * emb, axis=1, keepdims=True) + 1e-6)
    unit = emb * base_scale
    base_norm = (unit * gain_in[...]).astype(BF16).astype(F32)
    d_norm = jnp.zeros(emb.shape, F32)
    for k in range(n_taps):
        part = small[4 * k : 4 * k + 4, :]
        d_norm = d_norm + part * taps[k : k + 1, :]
        grad_conv[k : k + 1, :] = jnp.sum(part * base_norm, axis=0, keepdims=True)
    grad_gain[...] = jnp.sum(d_norm * unit, axis=0, keepdims=True)
    d_unit = d_norm * gain_in[...]
    base_sum = small[4 * n_taps : 4 * n_taps + 4, :]
    grad_emb[...] = base_sum + base_scale * (d_unit - unit * jnp.mean(d_unit * unit, axis=1, keepdims=True))
    grad_mid[...] = small[4 * n_taps + 8 : 4 * n_taps + 9, :]


def finish(small, embedding, gain_in, conv_taps):
    row = jax.ShapeDtypeStruct((1, embedding.shape[1]), F32)
    vmem = pl.BlockSpec(memory_space=pltpu.VMEM)
    grad_emb, grad_gain, grad_conv, grad_mid = pl.pallas_call(
        finish_kernel,
        out_shape=(jax.ShapeDtypeStruct(embedding.shape, F32), row, jax.ShapeDtypeStruct(conv_taps.shape[::-1], F32), row),
        in_specs=[vmem] * 4,
        out_specs=[vmem] * 4,
        name="finish",
    )(small, embedding, gain_in[None, :], conv_taps.T)
    return grad_emb, grad_gain[0], grad_conv.T, grad_mid[0]


MESH = pl.DeviceIdType.MESH


def greet(dp_peers, seq_peers):
    barrier = pltpu.get_barrier_semaphore()
    for peer in dp_peers:
        pl.semaphore_signal(barrier, inc=1, device_id=peer, device_id_type=MESH)
    for peer in seq_peers:
        pl.semaphore_signal(barrier, inc=1, device_id=peer, device_id_type=MESH)
    pl.semaphore_wait(barrier, len(dp_peers) + len(seq_peers))


def remote(src, dst, send, recv, peer):
    return pltpu.make_async_remote_copy(
        src_ref=src, dst_ref=dst, send_sem=send, recv_sem=recv, device_id=peer, device_id_type=MESH
    )


def ring_of(at, count, spot):
    return [spot(lax.rem(at + off, count)) for off in range(1, count)]


def gather_kernel(n_seq, shard, ids, gath, all_ids, send, recv, swap_send, swap_recv, id_send, id_recv):
    dp, sq = lax.axis_index("dp"), lax.axis_index("seq")
    core = lax.rem(dp, 2)
    mate = (dp + 1 - 2 * core, sq)
    peers = ring_of(sq, n_seq, lambda j: (dp, j))
    gath[sq] = shard[...].astype(BF16)
    wide = shard.shape[1] // 2
    low = pl.multiple_of(core * wide, wide)
    high = pl.multiple_of((1 - core) * wide, wide)
    greet([mate], peers)
    sends = []
    for off in range(1, n_seq):
        id_copy = remote(ids, all_ids.at[sq], id_send.at[off], id_recv.at[off], peers[off - 1])
        part = gath.at[sq, :, pl.ds(low, wide)]
        copy = remote(part, part, send.at[off], recv.at[off], peers[off - 1])
        id_copy.start()
        copy.start()
        sends += [id_copy, copy]
    all_ids[sq] = ids[...]
    for off in [*range(n_seq - 1, 0, -1)]:
        source = lax.rem(sq - off + n_seq, n_seq)
        landed = gath.at[source, :, pl.ds(low, wide)]
        remote(landed, landed, send.at[off], recv.at[off], mate).wait_recv()
        swap = remote(landed, landed, swap_send.at[off], swap_recv.at[off], mate)
        swap.start()
        sends.append(swap)
    for off in range(1, n_seq):
        source = lax.rem(sq - off + n_seq, n_seq)
        other = gath.at[source, :, pl.ds(high, wide)]
        remote(other, other, swap_send.at[off], swap_recv.at[off], mate).wait_recv()
        got = all_ids.at[source]
        remote(got, got, id_send.at[off], id_recv.at[off], mate).wait_recv()
    for copy in sends:
        copy.wait_send()


def gather_all(n_seq, shard, ids):
    rows, width = shard.shape
    vmem = pl.BlockSpec(memory_space=pltpu.VMEM)
    dma = pltpu.SemaphoreType.DMA((n_seq,))
    gath, all_ids = pl.pallas_call(
        lambda *refs: gather_kernel(n_seq, *refs),
        out_shape=(
            jax.ShapeDtypeStruct((n_seq, rows, width), BF16),
            jax.ShapeDtypeStruct((n_seq,) + ids.shape, ids.dtype),
        ),
        in_specs=[vmem] * 2,
        out_specs=[vmem] * 2,
        scratch_shapes=[dma] * 6,
        compiler_params=pltpu.CompilerParams(collective_id=0, has_side_effects=True),
        name="gather",
    )(shard, ids)
    return gath, all_ids


def at_axis(axis, index):
    return (slice(None),) * axis + (index,)


def reduce_kernel(n_dp, n_seq, mlp_a, mlp_b, filt, small, mlp_out, filt_out, small_out, *scratch):
    bits = n_dp.bit_length() - 1
    stages = bits
    per = 2 * stages
    rec_a, rec_b, rec_f = scratch[0:stages], scratch[stages:per], scratch[per : per + stages]
    rest = scratch[per + stages :]
    acc_a, acc_b, acc_f = rest[0:stages], rest[stages:per], rest[per : per + stages]
    small_acc, small_rec, z_mlp, z_mlp_rec, z_f_rec, z_s_rec, mine, gath = rest[per + stages : per + stages + 8]
    send, recv, z_send, z_recv, g_send, g_recv = rest[per + stages + 8 :]
    dp, sq = lax.axis_index("dp"), lax.axis_index("seq")
    dp_peers = ring_of(dp, n_dp, lambda i: (i, sq))
    seq_peers = ring_of(sq, n_seq, lambda j: (dp, j))
    greet(dp_peers, seq_peers)
    order_a = [*range(bits)]
    order_b = [0] + [*range(2, bits)] + ([1] if bits > 1 else [])
    left_a = [*range(bits - 1, -1, -1)]
    left_b = [*range(bits - 1, -1, -1)]
    cur_a, cur_b, cur_f, cur_s = mlp_a, mlp_b, filt, small
    waits = []
    for stage in range(stages):
        bit_a, bit_b = order_a[stage], order_b[stage]
        my_a, my_b = lax.rem(dp // 2**bit_a, 2), lax.rem(dp // 2**bit_b, 2)
        to_a = (dp + (1 - 2 * my_a) * 2**bit_a, sq)
        to_b = (dp + (1 - 2 * my_b) * 2**bit_b, sq)
        ax_a, ax_b = left_a.index(bit_a), left_b.index(bit_b)
        copies = [
            remote(cur_a.at[at_axis(ax_a, 1 - my_a)], rec_a[stage], send.at[stage, 0], recv.at[stage, 0], to_a),
            remote(cur_f.at[at_axis(ax_b, 1 - my_b)], rec_f[stage], send.at[stage, 1], recv.at[stage, 1], to_b),
            remote(cur_b.at[at_axis(ax_b, 1 - my_b)], rec_b[stage], send.at[stage, 2], recv.at[stage, 2], to_b),
            remote(cur_s, small_rec.at[stage], send.at[stage, 3], recv.at[stage, 3], to_a),
        ]
        for copy in copies:
            copy.start()
        waits += copies
        copies[0].wait_recv()
        acc_a[stage][...] = (cur_a[at_axis(ax_a, my_a)].astype(F32) + rec_a[stage][...].astype(F32)).astype(BF16)
        copies[1].wait_recv()
        acc_f[stage][...] = (cur_f[at_axis(ax_b, my_b)].astype(F32) + rec_f[stage][...].astype(F32)).astype(BF16)
        copies[2].wait_recv()
        acc_b[stage][...] = (cur_b[at_axis(ax_b, my_b)].astype(F32) + rec_b[stage][...].astype(F32)).astype(BF16)
        copies[3].wait_recv()
        small_acc[stage] = cur_s[...] + small_rec[stage]
        cur_a, cur_b, cur_f, cur_s = acc_a[stage], acc_b[stage], acc_f[stage], small_acc.at[stage]
        left_a.remove(bit_a)
        left_b.remove(bit_b)
    joined = jnp.concatenate([cur_a[...], cur_b[...]], 1)
    cols = joined.shape[1] // n_seq
    for j in range(n_seq):
        z_mlp[j] = joined[:, j * cols : (j + 1) * cols]
    for off in range(1, n_seq):
        to = lax.rem(sq + off, n_seq)
        copies = [
            remote(cur_f.at[to], z_f_rec.at[off], z_send.at[0, off], z_recv.at[0, off], (dp, to)),
            remote(cur_s, z_s_rec.at[sq], z_send.at[1, off], z_recv.at[1, off], (dp, to)),
            remote(z_mlp.at[to], z_mlp_rec.at[off], z_send.at[2, off], z_recv.at[2, off], (dp, to)),
        ]
        for copy in copies:
            copy.start()
        waits += copies
    z_s_rec[sq] = cur_s[...]
    total = cur_f[sq].astype(F32)
    for off in range(1, n_seq):
        slot = z_f_rec.at[off]
        remote(slot, slot, z_send.at[0, off], z_recv.at[0, off], (dp, sq)).wait_recv()
        total = total + z_f_rec[off].astype(F32)
    mine[...] = total.astype(BF16)
    for off in range(1, n_dp):
        to = lax.rem(dp + off, n_dp)
        copy = remote(mine, gath.at[dp], g_send.at[off], g_recv.at[off], (to, sq))
        copy.start()
        waits.append(copy)
    gath[dp] = mine[...]
    for off in range(1, n_seq):
        source = lax.rem(sq - off + n_seq, n_seq)
        slot = z_s_rec.at[source]
        remote(slot, slot, z_send.at[1, off], z_recv.at[1, off], (dp, sq)).wait_recv()
        slot = z_mlp_rec.at[off]
        remote(slot, slot, z_send.at[2, off], z_recv.at[2, off], (dp, sq)).wait_recv()
    total = z_mlp[sq].astype(F32)
    for off in range(1, n_seq):
        total = total + z_mlp_rec[off].astype(F32)
    mlp_out[...] = total
    total = z_s_rec[0]
    for j in range(1, n_seq):
        total = total + z_s_rec[j]
    small_out[...] = total
    for off in range(1, n_dp):
        source = lax.rem(dp - off + n_dp, n_dp)
        slot = gath.at[source]
        remote(slot, slot, g_send.at[off], g_recv.at[off], (dp, sq)).wait_recv()
    filt_out[...] = gath[...].astype(F32)
    for copy in waits:
        copy.wait_send()


def reduce_all(n_dp, n_seq, mlp_a, mlp_b, filt, small):
    bits = n_dp.bit_length() - 1
    twos = (2,) * bits
    lanes = 128
    rows, cut = mlp_a.shape
    width = cut + mlp_b.shape[1]
    part = rows // n_dp
    mlp_a = mlp_a.reshape(twos + (part, cut))
    mlp_b = mlp_b.reshape(twos + (part, width - cut))
    tidy = filt.ndim == 3
    chan = filt.shape[-2]
    length = filt.shape[-1] * (n_dp if tidy else 1)
    own = chan // n_seq
    if tidy:
        filt = filt.reshape(n_dp, n_seq, own, length // n_dp)
    else:
        filt = filt.reshape(n_seq, n_dp, -1, lanes).transpose(1, 0, 2, 3)
    f_tail = filt.shape[1:]
    filt = filt.reshape(twos + f_tail)

    def halves(tail):
        return [pltpu.VMEM(twos[stage + 1 :] + tail, BF16) for stage in range(bits)]

    tails = [(part, cut), (part, width - cut), f_tail]
    buffers = [b for tail in tails for b in halves(tail)]
    cols = width // n_seq
    dma = pltpu.SemaphoreType.DMA
    vmem = pl.BlockSpec(memory_space=pltpu.VMEM)
    mlp_out, filt_out, small_out = pl.pallas_call(
        lambda *refs: reduce_kernel(n_dp, n_seq, *refs),
        out_shape=(
            jax.ShapeDtypeStruct((part, cols), F32),
            jax.ShapeDtypeStruct((n_dp,) + f_tail[1:], F32),
            jax.ShapeDtypeStruct(small.shape, F32),
        ),
        in_specs=[vmem] * 4,
        out_specs=[vmem] * 3,
        scratch_shapes=buffers * 2
        + [
            pltpu.VMEM((bits,) + small.shape, F32),
            pltpu.VMEM((bits,) + small.shape, F32),
            pltpu.VMEM((n_seq, part, cols), BF16),
            pltpu.VMEM((n_seq, part, cols), BF16),
            pltpu.VMEM(f_tail, BF16),
            pltpu.VMEM((n_seq,) + small.shape, F32),
            pltpu.VMEM(f_tail[1:], BF16),
            pltpu.VMEM((n_dp,) + f_tail[1:], BF16),
            dma((bits, 4)),
            dma((bits, 4)),
            dma((3, n_seq)),
            dma((3, n_seq)),
            dma((n_dp,)),
            dma((n_dp,)),
        ],
        compiler_params=pltpu.CompilerParams(collective_id=1, has_side_effects=True, vmem_limit_bytes=32 * 2**20),
        name="reduce",
    )(mlp_a, mlp_b, filt, small)
    if tidy:
        filt_out = filt_out.transpose(1, 0, 2)
    return mlp_out, filt_out.reshape(own, length), small_out


def on_device(tokens, embedding, gain_in, conv_taps, long_filter, gain_mid, mlp_weights, cotangent):
    n_dp, n_seq = lax.axis_size("dp"), lax.axis_size("seq")
    filt, all_ids = gather_all(n_seq, long_filter, tokens)
    layer_out, mlp_a, mlp_b, grad_filter, small = compute(
        n_seq, n_dp, all_ids, tokens, embedding, gain_in, conv_taps, filt, gain_mid, mlp_weights, cotangent[0]
    )
    mlp_out, filter_out, small = reduce_all(n_dp, n_seq, mlp_a, mlp_b, grad_filter, small)
    grad_emb, grad_gain, grad_conv, grad_mid = finish(small, embedding, gain_in, conv_taps)
    return layer_out[None], grad_emb, grad_gain, grad_conv, filter_out, grad_mid, mlp_out


def solution(mesh):
    placed = (P("dp", "seq"), P(), P(), P(), P("seq", None), P(), P(), P("dp", None, "seq"))
    return jax.shard_map(
        on_device,
        mesh=mesh,
        in_specs=placed,
        out_specs=(P("dp", None, "seq"), P(), P(), P(), P("seq", None), P(), P("dp", "seq")),
        check_vma=False,
    )
```

profile of v0, /device:TPU:25, one launch (start us, length us, event | category | flops | bytes accessed | tf_op | source)
XLA Modules:
  0.0 75.8 jit_solution(7427972843116596725)
XLA Ops:
  0.6 0.7 broadcast_in_dim.10.gain_in
  1.3 0.0 copy-start.7
  1.3 0.7 broadcast_in_dim.11
  2.0 0.7 maximum_bitcast_fusion
  2.7 0.1 copy.17.refs_3_
  2.9 15.6 %gather.1 = (bf16[4,96,1024]{2,1,0:T(8,128)(2,1)}, s32[4,1,256]{2,1,0:T(1,128)}) custom-call(f32[96,1024]{1,0:T(8,128)} %refs_0_.1, s32[1,256]{1,0:T(1,128)} %refs_1_.3), custom_call_target="tpu_custom_call" | custom-call | tf_op jit(solution)/shard_map/gather/pallas_call | solution.py:283
  18.5 0.0 copy-start
  18.5 1.6 %copy-done = bf16[1024,1024]{1,0:T(8,128)(2,1)S(1)} copy-done((bf16[1024,1024]{1,0:T(8,128)(2,1)S(1)}, bf16[1024,1024]{1,0:T(8,128)(2,1)}, u32[]{:S(2)}) %copy-start) | copy-done | bytes 2097176
  20.1 0.0 copy-start.1
  20.1 1.5 %copy-done.1 = bf16[2304,384]{1,0:T(8,128)(2,1)S(1)} copy-done((bf16[2304,384]{1,0:T(8,128)(2,1)S(1)}, bf16[2304,384]{1,0:T(8,128)(2,1)}, u32[]{:S(2)}) %copy-start.1) | copy-done | bytes 1769496
  21.6 1.1 %copy-done.2 = bf16[4,96,1024]{2,1,0:T(8,128)(2,1)S(1)} copy-done((bf16[4,96,1024]{2,1,0:T(8,128)(2,1)S(1)}, bf16[4,96,1024]{2,1,0:T(8,128)(2,1)}, u32[]{:S(2)}) %copy-start.2) | copy-done | bytes 786456
  22.7 1.0 %copy-done.3 = bf16[1,768,256]{2,1,0:T(8,128)(2,1)S(1)} copy-done((bf16[1,768,256]{2,1,0:T(8,128)(2,1)S(1)}, bf16[1,768,256]{2,1,0:T(8,128)(2,1)}, u32[]{:S(2)}) %copy-start.3) | copy-done | bytes 393240
  23.7 0.7 copy-done.5
  24.4 0.7 copy-done.6
  25.1 7.1 %local.1 = (bf16[768,256]{1,0:T(8,128)(2,1)}, bf16[2304,256]{1,0:T(8,128)(2,1)S(1)}, bf16[2304,128]{1,0:T(8,128)(2,1)S(1)}, bf16[8,384,128]{2,1,0:T(8,128)(2,1)S(1)}, f32[32,384]{1,0:T(8,128)S(1)}) custom-call(s32[4,1,256]{2,1,0:T(1,128)S(1)} %copy-done.5, s32[1,256]{1,0:T(1,128)S(1)} %copy-done.6, bf16[1024,1024]{1,0:T(8,128)(2,1)S(1)} %copy-done, ...), custom_call_target="tpu_custom_call" | custom-call | tf_op jit(solution)/shard_map/local/pallas_call | solution.py:166
  32.1 0.0 copy-done.7
  32.1 37.4 %reduce.3 = (f32[288,96]{1,0:T(8,128)S(1)}, f32[8,96,128]{2,1,0:T(8,128)S(1)}, f32[32,384]{1,0:T(8,128)S(1)}) custom-call(bf16[2,2,2,288,256]{4,3,2,1,0:T(8,128)(2,1)S(1)} %bitcast.15, bf16[2,2,2,288,128]{4,3,2,1,0:T(8,128)(2,1)S(1)} %bitcast.17, bf16[2,2,2,4,96,128]{5,4,3,2,1,0:T(8,128)(2,1)S(1)} %bitcast.16, f32[32,384]{1,0:T(8,128)S(1)} %get-tuple-element.27.refs_3_), custom_call_target="tpu_custom_call" | custom-call | tf_op jit(solution)/shard_map/reduce/pallas_call | solution.py:425
  69.5 0.0 copy-start.4
  69.6 0.6 copy-done.4
  70.2 1.6 %finish.1 = (f32[4,384]{1,0:T(4,128)}, f32[1,384]{1,0:T(1,128)}, f32[4,384]{1,0:T(4,128)}, f32[1,384]{1,0:T(1,128)}) custom-call(f32[32,384]{1,0:T(8,128)} %copy-done.4, f32[4,384]{1,0:T(4,128)} %embedding.1, f32[1,384]{1,0:T(1,128)} %copy-done.7, f32[4,384]{1,0:T(4,128)} %bitcast.20), custom_call_target="tpu_custom_call" | custom-call | tf_op jit(solution)/shard_map/finish/pallas_call | solution.py:211
  71.8 1.3 %reduce.1 = f32[384]{0:T(512)} reduce(f32[1,384]{1,0:T(1,128)} %get-tuple-element.30, f32[]{:T(128)} %constant.5), dimensions={0}, to_apply=%get-tuple-element.30.reduce_sub_computation | reduce | bytes 3076 | tf_op jit(solution)/shard_map/finish/pallas_call | solution.py:211
  73.0 1.3 %reduce.2 = f32[384]{0:T(512)} reduce(f32[1,384]{1,0:T(1,128)} %get-tuple-element.33, f32[]{:T(128)} %constant.5), dimensions={0}, to_apply=%get-tuple-element.33.reduce_sub_computation | reduce | bytes 3076 | tf_op jit(solution)/shard_map/finish/pallas_call | solution.py:211
  74.3 0.8 %copy_bitcast_fusion = f32[96,1024]{1,0:T(8,128)} fusion(f32[8,96,128]{2,1,0:T(8,128)S(1)} %get-tuple-element.32), kind=kLoop, calls=%fused_computation | loop fusion | bytes 786432 | tf_op jit(solution)/shard_map/reshape | solution.py:456
  75.1 0.7 copy.22
  (4 shorter events, 0.0 us)
Async XLA Ops:
  1.3 30.8 %copy-start.7 = (f32[1,384]{1,0:T(1,128)}, f32[1,384]{1,0:T(1,128)S(1)}, u32[]{:S(2)}) copy-start(f32[1,384]{1,0:T(1,128)S(1)} %broadcast_in_dim.10.gain_in) | copy-start | bytes 4612
  18.5 1.6 %copy-start = (bf16[1024,1024]{1,0:T(8,128)(2,1)S(1)}, bf16[1024,1024]{1,0:T(8,128)(2,1)}, u32[]{:S(2)}) copy-start(bf16[1024,1024]{1,0:T(8,128)(2,1)} %constant.2.clone.refs_2_) | copy-start | bytes 6291460
  20.1 1.5 %copy-start.1 = (bf16[2304,384]{1,0:T(8,128)(2,1)S(1)}, bf16[2304,384]{1,0:T(8,128)(2,1)}, u32[]{:S(2)}) copy-start(bf16[2304,384]{1,0:T(8,128)(2,1)} %refs_5_.1) | copy-start | bytes 5308420
  21.6 1.1 %copy-start.2 = (bf16[4,96,1024]{2,1,0:T(8,128)(2,1)S(1)}, bf16[4,96,1024]{2,1,0:T(8,128)(2,1)}, u32[]{:S(2)}) copy-start(bf16[4,96,1024]{2,1,0:T(8,128)(2,1)} %get-tuple-element.22.refs_4_) | copy-start | bytes 2359300
  22.7 1.0 %copy-start.3 = (bf16[1,768,256]{2,1,0:T(8,128)(2,1)S(1)}, bf16[1,768,256]{2,1,0:T(8,128)(2,1)}, u32[]{:S(2)}) copy-start(bf16[1,768,256]{2,1,0:T(8,128)(2,1)} %param.16) | copy-start | bytes 1179652
  23.7 0.7 copy-start.5
  24.4 0.7 copy-start.6
  69.5 0.6 copy-start.4
where the time goes:
time: 76.3 us; the launch traced here: 75.8 us
  Pallas kernels  61.7 us (81%)
  local copies, waits for them, and re-layouts  10.1 us (13%)
  other arithmetic  3.27 us (4%)
    pallas_call x1, Pallas kernels, reduce_all(): pl.pallas_call(lambda *refs: reduce_kernel(n_dp, n_seq, *refs), out_shape...  37.4 us
    pallas_call x1, Pallas kernels, gather_all(): pl.pallas_call(lambda *refs: gather_kernel(n_seq, *refs), out_shape=(jax....  15.6 us
    unnamed x17, local copies, waits for them, and re-layouts  7.82 us
    pallas_call x1, Pallas kernels, compute(): pl.pallas_call(lambda *refs: local_kernel(n_seq, n_dp, tidy, *refs), out_...  7.05 us
    pallas_call x2, other arithmetic, finish(): pl.pallas_call(finish_kernel, out_shape=(jax.ShapeDtypeStruct(embedding.s...  2.55 us
    pallas_call x1, Pallas kernels, finish(): pl.pallas_call(finish_kernel, out_shape=(jax.ShapeDtypeStruct(embedding.s...  1.59 us

commit v1 on v0

v1 whole, which is shorter than its diff:
```python
import jax
import jax.numpy as jnp
import numpy as np
from jax import lax
from jax.experimental import pallas as pl
from jax.experimental.pallas import tpu as pltpu
from jax.sharding import PartitionSpec as P

F32 = jnp.float32
BF16 = jnp.bfloat16


def dct_table(length):
    freq = np.arange(length)[:, None]
    place = np.arange(length)[None, :]
    phase = (2 * place + 1) * freq % (4 * length)
    weight = np.where(freq == 0, np.sqrt(1.0 / length), np.sqrt(2.0 / length))
    return (weight * np.cos(np.pi * phase / (2 * length))).astype(np.float32).astype(BF16)


def dot(a, b, dims):
    return lax.dot_general(a, b, (dims, ((), ())), preferred_element_type=F32)


MESH = pl.DeviceIdType.MESH
TILE = 16


def flip(index, mask):
    bit = 1
    while bit <= mask:
        if mask & bit:
            index = index + bit * (1 - 2 * lax.rem(index // bit, 2))
        bit *= 2
    return index


def chunk_rows(part):
    units = part // TILE
    sizes = [TILE * ((units + 3 - i) // 4) for i in range(4)]
    sizes[3] += part - sum(sizes)
    return sizes


def stage_masks(order, stage, count):
    sent = [
        r
        for r in range(count)
        if (r >> order[stage]) & 1 and not any((r >> o) & 1 for o in order[:stage])
    ]
    return sorted(sent, key=lambda r: [-((r >> o) & 1) for o in order[stage + 1 :]])


class Sems:
    def __init__(self, send, recv):
        self.send, self.recv, self.used, self.started = send, recv, 0, []

    def take(self, count=1):
        first = self.used
        self.used += count
        return first

    def copy(self, index, src, dst, peer):
        return pltpu.make_async_remote_copy(
            src_ref=src,
            dst_ref=dst,
            send_sem=self.send.at[index],
            recv_sem=self.recv.at[index],
            device_id=peer,
            device_id_type=MESH,
        )

    def start(self, index, src, dst, peer):
        copy = self.copy(index, src, dst, peer)
        copy.start()
        self.started.append(copy)

    def arrived(self, index, dst, peer):
        self.copy(index, dst, dst, peer).wait_recv()

    def drain(self):
        for copy in self.started:
            copy.wait_send()


class Stream:
    def __init__(self, sems, order, place, recs):
        self.sems, self.order, self.place, self.recs = sems, order, place, recs
        self.count = 2 ** len(order)
        self.base = [sems.take(len(stage_masks(order, s, self.count))) for s in range(len(order))]

    def send_one(self, stage, mask, dp, sq):
        slot = stage_masks(self.order, stage, self.count).index(mask)
        peer = (flip(dp, 2 << self.order[stage]), sq)
        self.sems.start(
            self.base[stage] + slot, self.place(flip(dp // 2, mask)), self.recs[stage].at[slot], peer
        )

    def send_first(self, dp, sq, which):
        masks = stage_masks(self.order, 0, self.count)
        self.send_one(0, masks[which], dp, sq)

    def take_in(self, stage, dp, sq):
        for slot, mask in enumerate(stage_masks(self.order, stage, self.count)):
            kept = mask ^ (1 << self.order[stage])
            self.sems.arrived(self.base[stage] + slot, self.recs[stage].at[slot], (dp, sq))
            ref = self.place(flip(dp // 2, kept))
            ref[...] = (ref[...].astype(F32) + self.recs[stage][slot].astype(F32)).astype(BF16)
            if stage + 1 < len(self.order) and (kept >> self.order[stage + 1]) & 1:
                self.send_one(stage + 1, kept, dp, sq)


def sem_count(n_dp, n_seq, lanes_in):
    far, pairs = n_seq - 1, n_dp // 2
    bits = n_dp.bit_length() - 1
    return 2 * far + far * lanes_in + 4 * pairs + 2 + 6 * (pairs - 1) + bits + far + 6 * far + n_dp


def mega_kernel(
    n_dp, n_seq, lanes_in,
    ids, emb, gin, gmid, taps_in, shard, table_h, mlp_h, cot_h,
    out, mlp_out, filt_out, small_out,
    table, mlp, cot, gath, all_ids, full, spec_ref, level_ref, normed_ref, d_normed_ref, down_ref, d_act_ref,
    g0, g1, g2, g3, r0, r1, r2, r3, m0, m1, m2, m3,
    gf, rf, mf, z0, z1, z2, z3, y0, y1, y2, y3, yf, mine,
    sm, s_rec, s_acc, zs_rec,
    *rest,
):
    bits = n_dp.bit_length() - 1
    pairs = n_dp // 2
    stage_bufs = list(rest[: 6 * (bits - 1)])
    load_sem, send, recv = rest[6 * (bits - 1) :]
    sems = Sems(send, recv)
    grads, recs0, sums = (g0, g1, g2, g3), (r0, r1, r2, r3), (m0, m1, m2, m3)
    z_out, z_in = (z0, z1, z2, z3), (y0, y1, y2, y3)
    own_rows, block_len = shard.shape
    channels = own_rows * n_seq
    local_len = ids.shape[1]
    hidden = mlp.shape[0] // 3
    n_taps = taps_in.shape[0]
    half = 4 * n_taps
    part = mlp.shape[0] // n_dp
    sizes = chunk_rows(part)
    dp, sq = lax.axis_index("dp"), lax.axis_index("seq")
    core = lax.rem(dp, 2)
    me_q = dp // 2
    mate = (flip(dp, 1), sq)
    here = (dp, sq)
    wide = block_len // lanes_in
    lane_at = lax.rem(dp, lanes_in)

    loads = [
        pltpu.make_async_copy(table_h, table, load_sem.at[0]),
        pltpu.make_async_copy(cot_h, cot, load_sem.at[1]),
        pltpu.make_async_copy(mlp_h, mlp, load_sem.at[2]),
    ]
    for load in loads:
        load.start()
    barrier = pltpu.get_barrier_semaphore()
    for mask in range(1, n_dp):
        pl.semaphore_signal(barrier, inc=1, device_id=(flip(dp, mask), sq), device_id_type=MESH)
    for mask in range(1, n_seq):
        pl.semaphore_signal(barrier, inc=1, device_id=(dp, flip(sq, mask)), device_id_type=MESH)
    for p in range(lanes_in):
        gath[p, sq] = shard[:, p * wide : (p + 1) * wide].astype(BF16)
    all_ids[sq] = ids[...]
    pl.semaphore_wait(barrier, n_dp + n_seq - 2)

    id_base = sems.take(n_seq - 1)
    z_base = sems.take(n_seq - 1)
    for k in range(1, n_seq):
        to = (dp, flip(sq, k))
        sems.start(id_base + k - 1, ids, all_ids.at[sq], to)
        sems.start(z_base + k - 1, gath.at[lane_at, sq], gath.at[lane_at, sq], to)

    pad = 128 - 6 - n_taps
    rows_all = jnp.concatenate(
        [
            emb[...],
            gin[...].reshape(1, channels),
            gmid[...].reshape(1, channels),
            taps_in[...],
            jnp.zeros((pad, channels), F32),
        ],
        0,
    )
    packed = rows_all.T
    emb_cols, gain_in, gain_mid = packed[:, :4], packed[:, 4:5], packed[:, 5:6]
    taps = packed[:, 6 : 6 + n_taps]
    base_scale = lax.rsqrt(jnp.mean(emb_cols * emb_cols, axis=0, keepdims=True) + 1e-6)
    base_norm = (emb_cols * base_scale * gain_in).astype(BF16).astype(F32)
    lane = lax.broadcasted_iota(jnp.int32, (channels, half), 1)
    tap_part = jnp.zeros((channels, half), F32)
    base_part = jnp.zeros((channels, half), F32)
    for k in range(n_taps):
        tap_part = jnp.where(lane // 4 == k, taps[:, k : k + 1], tap_part)
    for a in range(4):
        base_part = jnp.where(lane % 4 == a, base_norm[:, a : a + 1], base_part)
    kmer = (tap_part * base_part).astype(BF16)
    turn = jnp.where(
        lax.broadcasted_iota(jnp.int32, (channels, channels), 0)
        + lax.broadcasted_iota(jnp.int32, (channels, channels), 1)
        == channels - 1,
        1.0,
        0.0,
    ).astype(BF16)
    loads[1].wait()
    turned = dot(turn, cot[channels:, :], ((1,), (0,))).astype(BF16)
    back = jnp.concatenate([cot[:channels, :], turned], 1)

    masks = [*range(2, lanes_in, 2)]
    near = [0] + masks if lanes_in > 1 else []
    far_base = sems.take((n_seq - 1) * len(masks))
    mate_base = sems.take((n_seq - 1) * len(near))

    def to_mate(k, n):
        piece = gath.at[flip(lane_at, near[n]), flip(sq, k)]
        sems.start(mate_base + (k - 1) * len(near) + n, piece, piece, mate)

    for k in range(1, n_seq):
        piece = gath.at[lane_at, flip(sq, k)]
        sems.arrived(z_base + k - 1, piece, here)
        for n, mask in enumerate(masks):
            sems.start(far_base + (k - 1) * len(masks) + n, piece, piece, (flip(dp, mask), sq))
        if near:
            to_mate(k, 0)
    for k in range(1, n_seq):
        sems.arrived(id_base + k - 1, all_ids.at[flip(sq, k)], here)

    per_block = block_len // local_len
    first = sq // per_block * per_block
    last = first + per_block - 1
    offset = pl.multiple_of((sq - first) * local_len, local_len)
    edge = 128
    before = jnp.where(first > 0, all_ids[jnp.maximum(first - 1, 0)][:, local_len - edge :], 4)
    after = jnp.where(last < n_seq - 1, all_ids[jnp.minimum(last + 1, n_seq - 1)][:, :edge], 4)
    row = jnp.concatenate([before] + [all_ids[first + j] for j in range(per_block)] + [after], 1)
    width = block_len + 2 * edge
    spread = jnp.broadcast_to(row, (8, width))
    sub = lax.broadcasted_iota(jnp.int32, (8, block_len), 0)
    tiles = []
    for s in range(2):
        for k in range(0, n_taps, 2):
            shifts = [(k + i) if s == 0 else (width - k - i) % width for i in range(2)]
            moved = [(pltpu.roll(spread, sh, 1) if sh else spread)[:, edge : edge + block_len] for sh in shifts]
            picked = jnp.where(sub < 4, moved[0], moved[1])
            want = sub % 4 if s == 0 else 3 - sub % 4
            tiles.append(jnp.where(picked == want, 1.0, 0.0))
    hot = jnp.concatenate(tiles, 0).astype(BF16)
    loads[0].wait()
    hot_spec = dot(hot, table[...], ((1,), (0,))).astype(BF16)
    for s in range(2):
        spec_ref[s] = dot(kmer, hot_spec[s * half : (s + 1) * half], ((1,), (0,))).astype(BF16)
    loads[2].wait()
    d_act_ref[...] = dot(mlp[2 * hidden :, :], back, ((1,), (0,)))

    for k in range(1, n_seq):
        for n, mask in enumerate(masks):
            piece = gath.at[flip(lane_at, mask), flip(sq, k)]
            sems.arrived(far_base + (k - 1) * len(masks) + n, piece, here)
            to_mate(k, n + 1)
    for k in range(1, n_seq):
        for n in range(len(near)):
            piece = gath.at[flip(lane_at, near[n] + 1), flip(sq, k)]
            sems.arrived(mate_base + (k - 1) * len(near) + n, piece, here)

    for p in range(lanes_in):
        full[:, p * wide : (p + 1) * wide] = gath[p].astype(F32).reshape(channels, wide)
    own = ids[...]
    q_own = table[pl.ds(offset, local_len), :]
    for s in range(2):
        scaled = (full[...] * spec_ref[s].astype(F32)).astype(BF16)
        mine_ids = own if s == 0 else 3 - own
        level = dot(scaled, q_own, ((1,), (1,)))
        residual = jnp.zeros((channels, local_len), F32)
        for a in range(4):
            residual = jnp.where(mine_ids == a, emb_cols[:, a : a + 1], residual)
        level_ref[:, s * local_len : (s + 1) * local_len] = level + residual
    level = level_ref[...]
    mid_scale = lax.rsqrt(jnp.mean(level * level, axis=0, keepdims=True) + 1e-6)
    normed_ref[...] = (level * mid_scale * gain_mid).astype(BF16)
    normed = normed_ref[...]

    edges = []
    for i in range(n_dp):
        at = i * part
        for c in range(4):
            edges.append((at, at + sizes[c], i, c))
            at += sizes[c]
    filled = {(i, c): 0 for i in range(n_dp) for c in range(4)}
    core_base = sems.take(4 * pairs)
    gone = set()

    def put(start, value):
        for lo, hi, i, c in edges:
            a, b = max(lo, start), min(hi, start + value.shape[0])
            if a < b:
                grads[c][i % 2, i // 2, a - lo : b - lo, :] = value[a - start : b - start, :]
                filled[i, c] += b - a

    def swap_done():
        for c in range(4):
            for q in range(pairs):
                if (c, q) not in gone and filled[2 * q, c] == sizes[c] and filled[2 * q + 1, c] == sizes[c]:
                    gone.add((c, q))
                    sems.start(core_base + c * pairs + q, grads[c].at[1 - core, q], recs0[c].at[q], mate)

    tile = 256 if hidden % 256 == 0 else hidden
    for t in range(hidden // tile):
        a0, u0, w0 = t * tile, hidden + t * tile, 2 * hidden + t * tile
        w_gate, w_up, w_down = mlp[a0 : a0 + tile, :], mlp[u0 : u0 + tile, :], mlp[w0 : w0 + tile, :]
        gate = dot(w_gate, normed, ((1,), (0,)))
        up = dot(w_up, normed, ((1,), (0,)))
        d_act = d_act_ref[a0 : a0 + tile, :]
        sig = jax.nn.sigmoid(gate)
        silu = gate * sig
        act = (silu * up).astype(BF16)
        d_gate = (d_act * up * (sig + silu * (1.0 - sig))).astype(BF16)
        d_up = (d_act * silu).astype(BF16)
        for start, left, right in ((a0, d_gate, normed), (u0, d_up, normed), (w0, act, back)):
            put(start, dot(left, right, ((1,), (1,))).astype(BF16))
        swap_done()
        down = dot(w_down, act, ((0,), (0,)))
        down_ref[...] = down if t == 0 else down_ref[...] + down
        d_part = dot(w_gate, d_gate, ((0,), (0,))) + dot(w_up, d_up, ((0,), (0,)))
        d_normed_ref[...] = d_part if t == 0 else d_normed_ref[...] + d_part

    order_a = [*range(bits - 1)]
    order_b = [*range(1, bits - 1)] + [0] if bits > 1 else []
    streams = []
    for c in range(4):
        recs = [stage_bufs[c * (bits - 1) + s] for s in range(bits - 1)]
        streams.append(Stream(sems, order_b if c % 2 else order_a, lambda q, c=c: sums[c].at[q], recs))
    split = n_seq // 2
    for c in range(2):
        recs = [stage_bufs[(4 + c) * (bits - 1) + s] for s in range(bits - 1)]
        lo, hi = (0, split) if c == 0 else (split, n_seq)
        streams.append(
            Stream(sems, order_b if c % 2 else order_a, lambda q, lo=lo, hi=hi: mf.at[q, pl.ds(lo, hi - lo)], recs)
        )
    n_first = len(stage_masks(order_a, 0, pairs)) if bits > 1 else 0

    def open_pair(lead):
        for c in (lead, lead + 1):
            for q in range(pairs):
                sems.arrived(core_base + c * pairs + q, recs0[c].at[q], here)
                sums[c][q] = (grads[c][core, q].astype(F32) + recs0[c][q].astype(F32)).astype(BF16)
        for which in range(n_first):
            for c in (lead, lead + 1):
                streams[c].send_first(dp, sq, which)

    def middle(lead):
        for stage in range(bits - 1):
            for c in (lead, lead + 1):
                streams[c].take_in(stage, dp, sq)

    cols = channels // n_seq
    zm_base = sems.take(4 * (n_seq - 1))

    def across(c):
        total = sums[c][me_q]
        for j in range(n_seq):
            z_out[c][j] = total[:, j * cols : (j + 1) * cols]
        for k in range(1, n_seq):
            sems.start(
                zm_base + c * (n_seq - 1) + k - 1, z_out[c].at[flip(sq, k)], z_in[c].at[k - 1], (dp, flip(sq, k))
            )

    open_pair(0)

    mid_level = level_ref[...]
    combined = (mid_level + down_ref[...]).astype(BF16)
    out[:channels, :] = combined[:, :local_len]
    out[channels:, :] = dot(turn, combined[:, local_len:], ((1,), (0,))).astype(BF16)
    unit = mid_level * mid_scale
    d_normed = d_normed_ref[...]
    mid_grad = d_normed * unit
    d_unit = d_normed * gain_mid
    d_level = back.astype(F32) + mid_scale * (d_unit - unit * jnp.mean(d_unit * unit, axis=0, keepdims=True))
    d_bf = d_level.astype(BF16)
    d_low = (d_level - d_bf.astype(F32)).astype(BF16)
    both = jnp.concatenate([own, 3 - own], 1)
    sub8 = lax.broadcasted_iota(jnp.int32, (8, 2 * local_len), 0)
    own_hot = jnp.where(sub8 == both, 1.0, 0.0).astype(BF16)
    ones = jnp.ones((8, 2 * local_len), BF16)
    m_bf = mid_grad.astype(BF16)
    m_low = (mid_grad - m_bf.astype(F32)).astype(BF16)
    base_part_sum = dot(own_hot, d_bf, ((1,), (1,))) + dot(own_hot, d_low, ((1,), (1,)))
    mid_part_sum = dot(ones, m_bf, ((1,), (1,))) + dot(ones, m_low, ((1,), (1,)))

    open_pair(2)

    grad_filter = jnp.zeros((channels, block_len), F32)
    kmer_sum = jnp.zeros((half, channels), F32)
    for s in range(2):
        d_scaled = dot(d_bf[:, s * local_len : (s + 1) * local_len], q_own, ((1,), (0,)))
        grad_filter = grad_filter + d_scaled * spec_ref[s].astype(F32)
        d_spec = (full[...] * d_scaled).astype(BF16)
        kmer_sum = kmer_sum + dot(hot_spec[s * half : (s + 1) * half], d_spec, ((1,), (1,)))
    grad_filter = grad_filter.astype(BF16)
    groups = n_dp // lanes_in
    piece_rows = own_rows // groups
    for i in range(n_dp):
        block = grad_filter[:, i % lanes_in * wide : (i % lanes_in + 1) * wide]
        for j in range(n_seq):
            top = j * own_rows + i // lanes_in * piece_rows
            gf[i % 2, i // 2, j] = block[top : top + piece_rows, :]
    rows_half = sm.shape[1]
    joined = jnp.concatenate([kmer_sum, base_part_sum, mid_part_sum], 0)
    sm[0] = joined[:rows_half]
    sm[1] = joined[rows_half:]
    f_base, s_base = sems.take(), sems.take(bits)
    sems.start(f_base, gf.at[1 - core], rf, mate)
    sems.start(s_base, sm.at[1 - core], s_rec.at[0], mate)

    middle(0)
    across(0)
    across(1)

    sems.arrived(f_base, rf, here)
    for q in range(pairs):
        mf[q] = (gf[core, q].astype(F32) + rf[q].astype(F32)).astype(BF16)
    for which in range(n_first):
        for c in (4, 5):
            streams[c].send_first(dp, sq, which)
    for b in range(bits):
        sems.arrived(s_base + b, s_rec.at[b], here)
        s_acc[b] = (sm[core] if b == 0 else s_acc[b - 1]) + s_rec[b]
        if b + 1 < bits:
            sems.start(s_base + b + 1, s_acc.at[b], s_rec.at[b + 1], (flip(dp, 2 << b), sq))
    zs_base = sems.take(n_seq - 1)
    zs_rec[sq] = s_acc[bits - 1]
    for k in range(1, n_seq):
        sems.start(zs_base + k - 1, s_acc.at[bits - 1], zs_rec.at[sq], (dp, flip(sq, k)))

    middle(4)
    zf_base = sems.take(n_seq - 1)
    for k in range(1, n_seq):
        sems.start(zf_base + k - 1, mf.at[me_q, flip(sq, k)], yf.at[k - 1], (dp, flip(sq, k)))
    middle(2)
    across(2)
    across(3)

    for k in range(1, n_seq):
        sems.arrived(zs_base + k - 1, zs_rec.at[flip(sq, k)], here)
    total = zs_rec[0]
    for j in range(1, n_seq):
        total = total + zs_rec[j]
    small_out[core] = total
    back_base = sems.take()
    sems.start(back_base, small_out.at[core], small_out.at[core], mate)

    total = mf[me_q, sq].astype(F32)
    for k in range(1, n_seq):
        sems.arrived(zf_base + k - 1, yf.at[k - 1], here)
        total = total + yf[k - 1].astype(F32)
    filt_out[dp] = total.astype(BF16)
    ring_base = sems.take(n_dp - 1)
    for mask in range(1, n_dp):
        sems.start(ring_base + mask - 1, filt_out.at[dp], filt_out.at[dp], (flip(dp, mask), sq))
    at = 0
    for c in range(4):
        total = z_out[c][sq].astype(F32)
        for k in range(1, n_seq):
            sems.arrived(zm_base + c * (n_seq - 1) + k - 1, z_in[c].at[k - 1], here)
            total = total + z_in[c][k - 1].astype(F32)
        mlp_out[at : at + sizes[c], :] = total
        at += sizes[c]
    sems.arrived(back_base, small_out.at[1 - core], here)
    for mask in range(1, n_dp):
        sems.arrived(ring_base + mask - 1, filt_out.at[flip(dp, mask)], here)
    sems.drain()


def finish_kernel(
    n_taps, layer, mlp_sum, filt, small, embedding, gain_in, taps,
    layer_out, grad_emb, grad_gain, grad_conv, filt_out, grad_mid, mlp_out,
):
    layer_out[...] = layer[...]
    mlp_out[...] = mlp_sum[...]
    n_dp, rows, wide = filt.shape
    lanes_in = filt_out.shape[1] // wide
    for i in range(n_dp):
        top, left = i // lanes_in * rows, i % lanes_in * wide
        filt_out[top : top + rows, left : left + wide] = filt[i].astype(F32)
    channels = embedding.shape[1]
    sums = jnp.concatenate([small[0], small[1]], 0)
    emb = embedding[...]
    gain = gain_in[...].reshape(1, channels)
    base_scale = lax.rsqrt(jnp.mean(emb * emb, axis=1, keepdims=True) + 1e-6)
    unit = emb * base_scale
    base_norm = (unit * gain).astype(BF16).astype(F32)
    d_norm = jnp.zeros(emb.shape, F32)
    for k in range(n_taps):
        part = sums[4 * k : 4 * k + 4, :]
        d_norm = d_norm + part * taps[k : k + 1, :]
        grad_conv[k : k + 1, :] = jnp.sum(part * base_norm, axis=0, keepdims=True)
    grad_gain[...] = jnp.sum(d_norm * unit, axis=0)
    d_unit = d_norm * gain
    base_sum = sums[4 * n_taps : 4 * n_taps + 4, :]
    grad_emb[...] = base_sum + base_scale * (d_unit - unit * jnp.mean(d_unit * unit, axis=1, keepdims=True))
    grad_mid[...] = sums[4 * n_taps + 8 : 4 * n_taps + 9, :].reshape(channels)


def on_device(tokens, embedding, gain_in, conv_taps, long_filter, gain_mid, mlp_weights, cotangent):
    n_dp, n_seq = lax.axis_size("dp"), lax.axis_size("seq")
    own_rows, block_len = long_filter.shape
    channels = own_rows * n_seq
    local_len = tokens.shape[1]
    lanes_in = n_dp
    while block_len % (lanes_in * 128):
        lanes_in //= 2
    wide = block_len // lanes_in
    table = jnp.asarray(dct_table(block_len).T)
    taps = conv_taps.T
    n_taps = taps.shape[0]
    pairs, bits = n_dp // 2, n_dp.bit_length() - 1
    part = mlp_weights.shape[0] // n_dp
    sizes = chunk_rows(part)
    cols = channels // n_seq
    piece = (own_rows // (n_dp // lanes_in), wide)
    rows_half = (4 * n_taps + 16) // 2
    orders = [[*range(bits - 1)], [*range(1, bits - 1)] + [0] if bits > 1 else []]
    two = 2 * local_len

    def v(shape, dtype=BF16):
        return pltpu.VMEM(shape, dtype)

    stage_bufs = []
    for c in range(6):
        order = orders[c % 2]
        split = n_seq // 2
        tail = (sizes[c], channels) if c < 4 else ((split if c == 4 else n_seq - split,) + piece)
        for s in range(bits - 1):
            stage_bufs.append(v((len(stage_masks(order, s, pairs)),) + tail))
    n_sems = sem_count(n_dp, n_seq, lanes_in)
    vmem = pl.BlockSpec(memory_space=pltpu.VMEM)
    hbm = pl.BlockSpec(memory_space=pltpu.HBM)
    cot = cotangent[0]
    layer, mlp_sum, filt, small = pl.pallas_call(
        lambda *refs: mega_kernel(n_dp, n_seq, lanes_in, *refs),
        out_shape=(
            jax.ShapeDtypeStruct(cot.shape, BF16),
            jax.ShapeDtypeStruct((part, cols), F32),
            jax.ShapeDtypeStruct((n_dp,) + piece, BF16),
            jax.ShapeDtypeStruct((2, rows_half, channels), F32),
        ),
        in_specs=[vmem] * 6 + [hbm] * 3,
        out_specs=[vmem] * 4,
        scratch_shapes=[
            v(table.shape),
            v(mlp_weights.shape),
            v(cot.shape),
            v((lanes_in, n_seq, own_rows, wide)),
            v((n_seq,) + tokens.shape, jnp.int32),
            v((channels, block_len), F32),
            v((2, channels, block_len)),
            v((channels, two), F32),
            v((channels, two)),
            v((channels, two), F32),
            v((channels, two), F32),
            v((mlp_weights.shape[0] // 3, two), F32),
        ]
        + [v((2, pairs, size, channels)) for size in sizes]
        + [v((pairs, size, channels)) for size in sizes]
        + [v((pairs, size, channels)) for size in sizes]
        + [v((2, pairs, n_seq) + piece), v((pairs, n_seq) + piece), v((pairs, n_seq) + piece)]
        + [v((n_seq, size, cols)) for size in sizes]
        + [v((n_seq - 1, size, cols)) for size in sizes]
        + [
            v((n_seq - 1,) + piece),
            v(piece),
            v((2, rows_half, channels), F32),
            v((bits, rows_half, channels), F32),
            v((bits, rows_half, channels), F32),
            v((n_seq, rows_half, channels), F32),
        ]
        + stage_bufs
        + [
            pltpu.SemaphoreType.DMA((3,)),
            pltpu.SemaphoreType.DMA((n_sems,)),
            pltpu.SemaphoreType.DMA((n_sems,)),
        ],
        compiler_params=pltpu.CompilerParams(
            collective_id=0, has_side_effects=True, vmem_limit_bytes=44 * 2**20
        ),
        name="mega",
    )(tokens, embedding, gain_in, gain_mid, taps, long_filter, table, mlp_weights, cot)
    layer_out, grad_emb, grad_gain, grad_conv, grad_filter, grad_mid, grad_mlp = pl.pallas_call(
        lambda *refs: finish_kernel(n_taps, *refs),
        out_shape=(
            jax.ShapeDtypeStruct(cot.shape, BF16),
            jax.ShapeDtypeStruct(embedding.shape, F32),
            jax.ShapeDtypeStruct(gain_in.shape, F32),
            jax.ShapeDtypeStruct(taps.shape, F32),
            jax.ShapeDtypeStruct(long_filter.shape, F32),
            jax.ShapeDtypeStruct(gain_mid.shape, F32),
            jax.ShapeDtypeStruct((part, cols), F32),
        ),
        in_specs=[vmem] * 7,
        out_specs=[vmem] * 7,
        name="finish",
    )(layer, mlp_sum, filt, small, embedding, gain_in, taps)
    return layer_out[None], grad_emb, grad_gain, grad_conv.T, grad_filter, grad_mid, grad_mlp


def solution(mesh):
    placed = (P("dp", "seq"), P(), P(), P(), P("seq", None), P(), P(), P("dp", None, "seq"))
    return jax.shard_map(
        on_device,
        mesh=mesh,
        in_specs=placed,
        out_specs=(P("dp", None, "seq"), P(), P(), P(), P("seq", None), P(), P("dp", "seq")),
        check_vma=False,
    )
```

time: 76.3 us -> 64.6 us (0.85)
  the two profiles are of different devices: /device:TPU:25 before, /device:TPU:0 now
where the time goes in v1:
time: 64.6 us; the launch traced here: 64.2 us
  Pallas kernels  52.3 us (81%)
  local copies, waits for them, and re-layouts  11.2 us (17%)
  between operations  0.67 us (1%)
    pallas_call x1, Pallas kernels, on_device(): pl.pallas_call(lambda *refs: mega_kernel(n_dp, n_seq, lanes_in, *refs), o...  50.1 us
    unnamed x26, local copies, waits for them, and re-layouts  11.2 us
    pallas_call x1, Pallas kernels, on_device(): pl.pallas_call(lambda *refs: finish_kernel(n_taps, *refs), out_shape=(jax...  2.23 us

profile of v1, /device:TPU:0, one launch (start us, length us, event | category | flops | bytes accessed | tf_op | source)
XLA Modules:
  0.0 64.2 jit_solution(5137818692601087295)
XLA Ops:
  0.6 0.0 copy-start
  0.6 1.6 %copy-done = bf16[1024,1024]{1,0:T(8,128)(2,1)S(1)} copy-done((bf16[1024,1024]{1,0:T(8,128)(2,1)S(1)}, bf16[1024,1024]{1,0:T(8,128)(2,1)}, u32[]{:S(2)}) %copy-start) | copy-done | bytes 2097176
  2.2 0.0 copy-start.1
  2.2 1.5 %copy-done.1 = bf16[2304,384]{1,0:T(8,128)(2,1)S(1)} copy-done((bf16[2304,384]{1,0:T(8,128)(2,1)S(1)}, bf16[2304,384]{1,0:T(8,128)(2,1)}, u32[]{:S(2)}) %copy-start.1) | copy-done | bytes 1769496
  3.7 0.0 copy-start.2
  3.7 1.0 %copy-done.2 = f32[96,1024]{1,0:T(8,128)S(1)} copy-done((f32[96,1024]{1,0:T(8,128)S(1)}, f32[96,1024]{1,0:T(8,128)}, u32[]{:S(2)}) %copy-start.2) | copy-done | bytes 393240
  4.7 0.0 copy-start.3
  4.7 1.0 %copy-done.3 = bf16[1,768,256]{2,1,0:T(8,128)(2,1)S(1)} copy-done((bf16[1,768,256]{2,1,0:T(8,128)(2,1)S(1)}, bf16[1,768,256]{2,1,0:T(8,128)(2,1)}, u32[]{:S(2)}) %copy-start.3) | copy-done | bytes 393240
  5.7 0.0 copy-start.8
  5.7 0.7 %copy-done.8 = f32[4,384]{1,0:T(4,128)S(1)} copy-done((f32[4,384]{1,0:T(4,128)S(1)}, f32[4,384]{1,0:T(4,128)}, u32[]{:S(2)}) %copy-start.8) | copy-done | bytes 6168
  6.4 0.0 copy-start.9
  6.4 0.7 %copy-done.9 = f32[384,4]{0,1:T(4,128)S(1)} copy-done((f32[384,4]{0,1:T(4,128)S(1)}, f32[384,4]{0,1:T(4,128)}, u32[]{:S(2)}) %copy-start.9) | copy-done | bytes 6168
  7.1 0.0 copy-start.10
  7.1 0.7 %copy-done.10 = f32[384]{0:T(512)S(1)} copy-done((f32[384]{0:T(512)S(1)}, f32[384]{0:T(512)}, u32[]{:S(2)}) %copy-start.10) | copy-done | bytes 1560
  7.8 0.0 copy-start.11
  7.8 0.7 %copy-done.11 = f32[384]{0:T(512)S(1)} copy-done((f32[384]{0:T(512)S(1)}, f32[384]{0:T(512)}, u32[]{:S(2)}) %copy-start.11) | copy-done | bytes 1560
  8.4 0.7 %copy-done.12 = s32[1,256]{1,0:T(1,128)S(1)} copy-done((s32[1,256]{1,0:T(1,128)S(1)}, s32[1,256]{1,0:T(1,128)}, u32[]{:S(2)}) %copy-start.12) | copy-done | bytes 1048
  9.1 50.1 %mega.1 = (bf16[768,256]{1,0:T(8,128)(2,1)S(1)}, f32[288,96]{1,0:T(8,128)S(1)}, bf16[8,96,128]{2,1,0:T(8,128)(2,1)S(1)}, f32[2,16,384]{2,1,0:T(8,128)S(1)}) custom-call(s32[1,256]{1,0:T(1,128)S(1)} %copy-done.12, f32[4,384]{1,0:T(4,128)S(1)} %copy-done.8, f32[384]{0:T(512)S(1)} %copy-done.10, f32[384]{0:T(512)S(1)} %copy-done.11, f32[4,384]{1,0:T(4,128)S(1)} %bitcast.6, ...), custom_call_target="tpu_custom_call" | custom-call | tf_op jit(solution)/shard_map/mega/pallas_call | solution.py:540
  59.2 0.0 copy-start.4
  59.2 0.7 %copy-done.4 = bf16[768,256]{1,0:T(8,128)(2,1)} copy-done((bf16[768,256]{1,0:T(8,128)(2,1)}, bf16[768,256]{1,0:T(8,128)(2,1)S(1)}, u32[]{:S(2)}) %copy-start.4) | copy-done | bytes 393240
  60.0 0.7 %copy-done.5 = bf16[8,96,128]{2,1,0:T(8,128)(2,1)} copy-done((bf16[8,96,128]{2,1,0:T(8,128)(2,1)}, bf16[8,96,128]{2,1,0:T(8,128)(2,1)S(1)}, u32[]{:S(2)}) %copy-start.5) | copy-done | bytes 196632
  60.6 0.7 %copy-done.6 = f32[288,96]{1,0:T(8,128)} copy-done((f32[288,96]{1,0:T(8,128)}, f32[288,96]{1,0:T(8,128)S(1)}, u32[]{:S(2)}) %copy-start.6) | copy-done | bytes 110616
  61.3 0.6 copy-done.7
  61.9 2.2 %finish.1 = (bf16[768,256]{1,0:T(8,128)(2,1)}, f32[4,384]{1,0:T(4,128)}, f32[384]{0:T(512)}, f32[4,384]{1,0:T(4,128)}, f32[96,1024]{1,0:T(8,128)}, /*index=5*/f32[384]{0:T(512)}, f32[288,96]{1,0:T(8,128)}) custom-call(bf16[768,256]{1,0:T(8,128)(2,1)} %copy-done.4, f32[288,96]{1,0:T(8,128)} %copy-done.6, bf16[8,96,128]{2,1,0:T(8,128)(2,1)} %copy-done.5, ...), custom_call_target="tpu_custom_call" | custom-call | tf_op jit(solution)/shard_map/finish/pallas_call | solution.py:589
  (4 shorter events, 0.0 us)
Async XLA Ops:
  0.6 1.6 %copy-start = (bf16[1024,1024]{1,0:T(8,128)(2,1)S(1)}, bf16[1024,1024]{1,0:T(8,128)(2,1)}, u32[]{:S(2)}) copy-start(bf16[1024,1024]{1,0:T(8,128)(2,1)} %constant.2.clone.refs_6_) | copy-start | bytes 6291460
  2.2 1.5 %copy-start.1 = (bf16[2304,384]{1,0:T(8,128)(2,1)S(1)}, bf16[2304,384]{1,0:T(8,128)(2,1)}, u32[]{:S(2)}) copy-start(bf16[2304,384]{1,0:T(8,128)(2,1)} %refs_7_.1) | copy-start | bytes 5308420
  3.7 1.0 %copy-start.2 = (f32[96,1024]{1,0:T(8,128)S(1)}, f32[96,1024]{1,0:T(8,128)}, u32[]{:S(2)}) copy-start(f32[96,1024]{1,0:T(8,128)} %refs_5_.2) | copy-start | bytes 1179652
  4.7 1.0 %copy-start.3 = (bf16[1,768,256]{2,1,0:T(8,128)(2,1)S(1)}, bf16[1,768,256]{2,1,0:T(8,128)(2,1)}, u32[]{:S(2)}) copy-start(bf16[1,768,256]{2,1,0:T(8,128)(2,1)} %param.16) | copy-start | bytes 1179652
  5.7 0.7 %copy-start.8 = (f32[4,384]{1,0:T(4,128)S(1)}, f32[4,384]{1,0:T(4,128)}, u32[]{:S(2)}) copy-start(f32[4,384]{1,0:T(4,128)} %refs_4_.1) | copy-start | bytes 18436
  6.4 0.7 %copy-start.9 = (f32[384,4]{0,1:T(4,128)S(1)}, f32[384,4]{0,1:T(4,128)}, u32[]{:S(2)}) copy-start(f32[384,4]{0,1:T(4,128)} %param.12) | copy-start | bytes 18436
  7.1 0.7 %copy-start.10 = (f32[384]{0:T(512)S(1)}, f32[384]{0:T(512)}, u32[]{:S(2)}) copy-start(f32[384]{0:T(512)} %refs_5_.3) | copy-start | bytes 4612
  7.8 0.7 %copy-start.11 = (f32[384]{0:T(512)S(1)}, f32[384]{0:T(512)}, u32[]{:S(2)}) copy-start(f32[384]{0:T(512)} %refs_3_.1) | copy-start | bytes 4612
  8.4 0.7 %copy-start.12 = (s32[1,256]{1,0:T(1,128)S(1)}, s32[1,256]{1,0:T(1,128)}, u32[]{:S(2)}) copy-start(s32[1,256]{1,0:T(1,128)} %refs_0_.1) | copy-start | bytes 3076
  59.2 0.7 %copy-start.4 = (bf16[768,256]{1,0:T(8,128)(2,1)}, bf16[768,256]{1,0:T(8,128)(2,1)S(1)}, u32[]{:S(2)}) copy-start(bf16[768,256]{1,0:T(8,128)(2,1)S(1)} %get-tuple-element.18.refs_0_) | copy-start | bytes 1179652
  60.0 0.7 %copy-start.5 = (bf16[8,96,128]{2,1,0:T(8,128)(2,1)}, bf16[8,96,128]{2,1,0:T(8,128)(2,1)S(1)}, u32[]{:S(2)}) copy-start(bf16[8,96,128]{2,1,0:T(8,128)(2,1)S(1)} %get-tuple-element.20.refs_2_) | copy-start | bytes 589828
  60.6 0.7 %copy-start.6 = (f32[288,96]{1,0:T(8,128)}, f32[288,96]{1,0:T(8,128)S(1)}, u32[]{:S(2)}) copy-start(f32[288,96]{1,0:T(8,128)S(1)} %get-tuple-element.19.refs_1_) | copy-start | bytes 331780
  61.3 0.6 copy-start.7

commit v2 on v1

--- a/solution.py
+++ b/solution.py
@@ -582,7 +582,7 @@
             pltpu.SemaphoreType.DMA((n_sems,)),
         ],
         compiler_params=pltpu.CompilerParams(
-            collective_id=0, has_side_effects=True, vmem_limit_bytes=44 * 2**20
+            collective_id=0, has_side_effects=True, vmem_limit_bytes=62 * 2**20
         ),
         name="mega",
     )(tokens, embedding, gain_in, gain_mid, taps, long_filter, table, mlp_weights, cot)
@@ -599,6 +599,7 @@
         ),
         in_specs=[vmem] * 7,
         out_specs=[vmem] * 7,
+        compiler_params=pltpu.CompilerParams(vmem_limit_bytes=62 * 2**20),
         name="finish",
     )(layer, mlp_sum, filt, small, embedding, gain_in, taps)
     return layer_out[None], grad_emb, grad_gain, grad_conv.T, grad_filter, grad_mid, grad_mlp

time: 64.6 us -> 54.3 us (0.84)
  local copies, waits for them, and re-layouts: 11.2 us -> 0 us
  Pallas kernels: 52.3 us -> 53.5 us
    unnamed x26 -> x0, local copies, waits for them, and re-layouts: 11.2 us -> none
    pallas_call x1, Pallas kernels: 50.1 us -> 51.3 us  [on_device(): pl.pallas_call(lambda *refs: mega_kernel(n_dp, n_seq, lanes_in, *refs), o...]
where the time goes in v2:
time: 54.3 us; the launch traced here: 54.1 us
  Pallas kernels  53.5 us (99%)
  between operations  0.64 us (1%)
    pallas_call x1, Pallas kernels, on_device(): pl.pallas_call(lambda *refs: mega_kernel(n_dp, n_seq, lanes_in, *refs), o...  51.3 us
    pallas_call x1, Pallas kernels, on_device(): pl.pallas_call(lambda *refs: finish_kernel(n_taps, *refs), out_shape=(jax...  2.24 us

profile of v2, /device:TPU:0, one launch (start us, length us, event | category | flops | bytes accessed | tf_op | source)
XLA Modules:
  0.0 54.1 jit_solution(10734428191585263358)
XLA Ops:
  0.6 51.3 %mega.1 = (bf16[768,256]{1,0:T(8,128)(2,1)}, f32[288,96]{1,0:T(8,128)}, bf16[8,96,128]{2,1,0:T(8,128)(2,1)}, f32[2,16,384]{2,1,0:T(8,128)}) custom-call(s32[1,256]{1,0:T(1,128)} %refs_0_.1, f32[4,384]{1,0:T(4,128)} %refs_4_.1, f32[384]{0:T(512)} %refs_5_.3, f32[384]{0:T(512)} %refs_3_.1, f32[4,384]{1,0:T(4,128)} %bitcast.5, f32[96,1024]{1,0:T(8,128)} %refs_5_.2, ...), custom_call_target="tpu_custom_call" | custom-call | tf_op jit(solution)/shard_map/mega/pallas_call | solution.py:540
  51.9 2.2 %finish.1 = (bf16[768,256]{1,0:T(8,128)(2,1)}, f32[4,384]{1,0:T(4,128)}, f32[384]{0:T(512)}, f32[4,384]{1,0:T(4,128)}, f32[96,1024]{1,0:T(8,128)}, /*index=5*/f32[384]{0:T(512)}, f32[288,96]{1,0:T(8,128)}) custom-call(bf16[768,256]{1,0:T(8,128)(2,1)} %get-tuple-element.18.refs_0_, f32[288,96]{1,0:T(8,128)} %get-tuple-element.19.refs_1_, ...), custom_call_target="tpu_custom_call" | custom-call | tf_op jit(solution)/shard_map/finish/pallas_call | solution.py:589

commit v3 on v2

--- a/solution.py
+++ b/solution.py
@@ -1,3 +1,5 @@
+import math
+
 import jax
 import jax.numpy as jnp
 import numpy as np
@@ -23,7 +25,7 @@
 
 
 MESH = pl.DeviceIdType.MESH
-TILE = 16
+N_TILES = 3
 
 
 def flip(index, mask):
@@ -35,11 +37,37 @@
     return index
 
 
-def chunk_rows(part):
-    units = part // TILE
-    sizes = [TILE * ((units + 3 - i) // 4) for i in range(4)]
-    sizes[3] += part - sum(sizes)
-    return sizes
+def row_group(part, hidden):
+    return math.gcd(part, hidden) // N_TILES
+
+
+def color_rows(rows):
+    return rows // 32 * 16 or 8
+
+
+def pack_rows(rows, cols):
+    spare = 128 - cols
+    if spare <= 0 or cols % spare or rows % (8 * (cols // spare + 1)):
+        return 0
+    return rows * cols // 128
+
+
+def pack(block):
+    rows, cols = block.shape
+    main = pack_rows(rows, cols)
+    if not main:
+        return block
+    spare = 128 - cols
+    rest = jnp.concatenate([block[main:, at : at + spare] for at in range(0, cols, spare)], 0)
+    return jnp.concatenate([block[:main], rest], 1)
+
+
+def unpack(block, rows, cols):
+    main = pack_rows(rows, cols)
+    if not main:
+        return block
+    rest = jnp.concatenate([block[at : at + rows - main, cols:] for at in range(0, main, rows - main)], 1)
+    return jnp.concatenate([block[:, :cols], rest], 0)
 
 
 def stage_masks(order, stage, count):
@@ -113,7 +141,7 @@
 def sem_count(n_dp, n_seq, lanes_in):
     far, pairs = n_seq - 1, n_dp // 2
     bits = n_dp.bit_length() - 1
-    return 2 * far + far * lanes_in + 4 * pairs + 2 + 6 * (pairs - 1) + bits + far + 6 * far + n_dp
+    return 2 * far + far * lanes_in + N_TILES + 2 + 8 * (pairs - 1) + bits + far + 6 * far + n_dp
 
 
 def mega_kernel(
@@ -121,18 +149,15 @@
     ids, emb, gin, gmid, taps_in, shard, table_h, mlp_h, cot_h,
     out, mlp_out, filt_out, small_out,
     table, mlp, cot, gath, all_ids, full, spec_ref, level_ref, normed_ref, d_normed_ref, down_ref, d_act_ref,
-    g0, g1, g2, g3, r0, r1, r2, r3, m0, m1, m2, m3,
-    gf, rf, mf, z0, z1, z2, z3, y0, y1, y2, y3, yf, mine,
+    grads, recs0, sums, z_out, z_in, keep, gf, rf, mf, yf,
     sm, s_rec, s_acc, zs_rec,
     *rest,
 ):
     bits = n_dp.bit_length() - 1
     pairs = n_dp // 2
-    stage_bufs = list(rest[: 6 * (bits - 1)])
-    load_sem, send, recv = rest[6 * (bits - 1) :]
+    stage_bufs = list(rest[: 8 * (bits - 1)])
+    load_sem, send, recv = rest[8 * (bits - 1) :]
     sems = Sems(send, recv)
-    grads, recs0, sums = (g0, g1, g2, g3), (r0, r1, r2, r3), (m0, m1, m2, m3)
-    z_out, z_in = (z0, z1, z2, z3), (y0, y1, y2, y3)
     own_rows, block_len = shard.shape
     channels = own_rows * n_seq
     local_len = ids.shape[1]
@@ -140,7 +165,9 @@
     n_taps = taps_in.shape[0]
     half = 4 * n_taps
     part = mlp.shape[0] // n_dp
-    sizes = chunk_rows(part)
+    group = row_group(part, hidden)
+    span = N_TILES * group
+    chunk = part // N_TILES
     dp, sq = lax.axis_index("dp"), lax.axis_index("seq")
     core = lax.rem(dp, 2)
     me_q = dp // 2
@@ -252,7 +279,11 @@
     for s in range(2):
         spec_ref[s] = dot(kmer, hot_spec[s * half : (s + 1) * half], ((1,), (0,))).astype(BF16)
     loads[2].wait()
-    d_act_ref[...] = dot(mlp[2 * hidden :, :], back, ((1,), (0,)))
+    for t in range(N_TILES):
+        w_down = jnp.concatenate(
+            [mlp[2 * hidden + h * span + t * group : 2 * hidden + h * span + (t + 1) * group, :] for h in range(hidden // span)], 0
+        )
+        d_act_ref[t] = dot(w_down, back, ((1,), (0,)))
 
     for k in range(1, n_seq):
         for n, mask in enumerate(masks):
@@ -281,114 +312,95 @@
     normed_ref[...] = (level * mid_scale * gain_mid).astype(BF16)
     normed = normed_ref[...]
 
-    edges = []
-    for i in range(n_dp):
-        at = i * part
-        for c in range(4):
-            edges.append((at, at + sizes[c], i, c))
-            at += sizes[c]
-    filled = {(i, c): 0 for i in range(n_dp) for c in range(4)}
-    core_base = sems.take(4 * pairs)
-    gone = set()
-
-    def put(start, value):
-        for lo, hi, i, c in edges:
-            a, b = max(lo, start), min(hi, start + value.shape[0])
-            if a < b:
-                grads[c][i % 2, i // 2, a - lo : b - lo, :] = value[a - start : b - start, :]
-                filled[i, c] += b - a
-
-    def swap_done():
-        for c in range(4):
-            for q in range(pairs):
-                if (c, q) not in gone and filled[2 * q, c] == sizes[c] and filled[2 * q + 1, c] == sizes[c]:
-                    gone.add((c, q))
-                    sems.start(core_base + c * pairs + q, grads[c].at[1 - core, q], recs0[c].at[q], mate)
-
-    tile = 256 if hidden % 256 == 0 else hidden
-    for t in range(hidden // tile):
-        a0, u0, w0 = t * tile, hidden + t * tile, 2 * hidden + t * tile
-        w_gate, w_up, w_down = mlp[a0 : a0 + tile, :], mlp[u0 : u0 + tile, :], mlp[w0 : w0 + tile, :]
+    order_a = [*range(bits - 1)]
+    order_b = [*range(1, bits - 1)] + [0] if bits > 1 else []
+    streams = []
+    upper = color_rows(chunk)
+    split = n_seq // 2
+
+    def bufs_of(index):
+        return stage_bufs[index * (bits - 1) : (index + 1) * (bits - 1)]
+
+    for t in range(N_TILES):
+        for c, (lo, hi) in enumerate(((0, upper), (upper, chunk))):
+            place = lambda q, t=t, lo=lo, hi=hi: sums.at[t, q, pl.ds(lo, hi - lo)]
+            streams.append(Stream(sems, order_b if c else order_a, place, bufs_of(2 * t + c)))
+    for c, (lo, hi) in enumerate(((0, split), (split, n_seq))):
+        place = lambda q, lo=lo, hi=hi: mf.at[q, pl.ds(lo, hi - lo)]
+        streams.append(Stream(sems, order_b if c else order_a, place, bufs_of(2 * N_TILES + c)))
+    n_first = len(stage_masks(order_a, 0, pairs)) if bits > 1 else 0
+    core_base = sems.take(N_TILES)
+    zm_base = sems.take(N_TILES * (n_seq - 1))
+    cols = channels // n_seq
+
+    def put(t, base, value):
+        for h in range(hidden // span):
+            start = base + span * h
+            i, j = start // part, start % part // span
+            grads[t, i % 2, i // 2, j * group : (j + 1) * group, :] = value[h * group : (h + 1) * group, :]
+
+    def swap(t, d_gate, d_up, act):
+        for base, left, right in ((0, d_gate, normed), (hidden, d_up, normed), (2 * hidden, act, back)):
+            put(t, base, dot(left, right, ((1,), (1,))).astype(BF16))
+        sems.start(core_base + t, grads.at[t, 1 - core], recs0.at[t], mate)
+
+    def launch(lead):
+        for which in range(n_first):
+            for c in (lead, lead + 1):
+                streams[c].send_first(dp, sq, which)
+
+    def open_chunk(t):
+        sems.arrived(core_base + t, recs0.at[t], here)
+        for q in range(pairs):
+            sums[t, q] = (grads[t, core, q].astype(F32) + recs0[t, q].astype(F32)).astype(BF16)
+        launch(2 * t)
+
+    def take_in(lead, stages):
+        for stage in stages:
+            for c in (lead, lead + 1):
+                streams[c].take_in(stage, dp, sq)
+
+    def across(t):
+        total = sums[t, me_q].astype(F32)
+        for j in range(n_seq):
+            z_out[t, j] = pack(total[:, j * cols : (j + 1) * cols]).astype(BF16)
+        for k in range(1, n_seq):
+            to = flip(sq, k)
+            sems.start(zm_base + t * (n_seq - 1) + k - 1, z_out.at[t, to], z_in.at[t, k - 1], (dp, to))
+
+    def rows_of(base, t):
+        return jnp.concatenate(
+            [mlp[base + h * span + t * group : base + h * span + (t + 1) * group, :] for h in range(hidden // span)], 0
+        )
+
+    for t in range(N_TILES):
+        w_gate, w_up, w_down = rows_of(0, t), rows_of(hidden, t), rows_of(2 * hidden, t)
         gate = dot(w_gate, normed, ((1,), (0,)))
         up = dot(w_up, normed, ((1,), (0,)))
-        d_act = d_act_ref[a0 : a0 + tile, :]
+        d_act = d_act_ref[t]
         sig = jax.nn.sigmoid(gate)
         silu = gate * sig
         act = (silu * up).astype(BF16)
         d_gate = (d_act * up * (sig + silu * (1.0 - sig))).astype(BF16)
         d_up = (d_act * silu).astype(BF16)
-        for start, left, right in ((a0, d_gate, normed), (u0, d_up, normed), (w0, act, back)):
-            put(start, dot(left, right, ((1,), (1,))).astype(BF16))
-        swap_done()
+        if t > 0:
+            open_chunk(t - 1)
+        if t + 1 < N_TILES:
+            swap(t, d_gate, d_up, act)
+        else:
+            keep[0], keep[1], keep[2] = d_gate, d_up, act
         down = dot(w_down, act, ((0,), (0,)))
         down_ref[...] = down if t == 0 else down_ref[...] + down
         d_part = dot(w_gate, d_gate, ((0,), (0,))) + dot(w_up, d_up, ((0,), (0,)))
         d_normed_ref[...] = d_part if t == 0 else d_normed_ref[...] + d_part
 
-    order_a = [*range(bits - 1)]
-    order_b = [*range(1, bits - 1)] + [0] if bits > 1 else []
-    streams = []
-    for c in range(4):
-        recs = [stage_bufs[c * (bits - 1) + s] for s in range(bits - 1)]
-        streams.append(Stream(sems, order_b if c % 2 else order_a, lambda q, c=c: sums[c].at[q], recs))
-    split = n_seq // 2
-    for c in range(2):
-        recs = [stage_bufs[(4 + c) * (bits - 1) + s] for s in range(bits - 1)]
-        lo, hi = (0, split) if c == 0 else (split, n_seq)
-        streams.append(
-            Stream(sems, order_b if c % 2 else order_a, lambda q, lo=lo, hi=hi: mf.at[q, pl.ds(lo, hi - lo)], recs)
-        )
-    n_first = len(stage_masks(order_a, 0, pairs)) if bits > 1 else 0
-
-    def open_pair(lead):
-        for c in (lead, lead + 1):
-            for q in range(pairs):
-                sems.arrived(core_base + c * pairs + q, recs0[c].at[q], here)
-                sums[c][q] = (grads[c][core, q].astype(F32) + recs0[c][q].astype(F32)).astype(BF16)
-        for which in range(n_first):
-            for c in (lead, lead + 1):
-                streams[c].send_first(dp, sq, which)
-
-    def middle(lead):
-        for stage in range(bits - 1):
-            for c in (lead, lead + 1):
-                streams[c].take_in(stage, dp, sq)
-
-    cols = channels // n_seq
-    zm_base = sems.take(4 * (n_seq - 1))
-
-    def across(c):
-        total = sums[c][me_q]
-        for j in range(n_seq):
-            z_out[c][j] = total[:, j * cols : (j + 1) * cols]
-        for k in range(1, n_seq):
-            sems.start(
-                zm_base + c * (n_seq - 1) + k - 1, z_out[c].at[flip(sq, k)], z_in[c].at[k - 1], (dp, flip(sq, k))
-            )
-
-    open_pair(0)
-
     mid_level = level_ref[...]
-    combined = (mid_level + down_ref[...]).astype(BF16)
-    out[:channels, :] = combined[:, :local_len]
-    out[channels:, :] = dot(turn, combined[:, local_len:], ((1,), (0,))).astype(BF16)
     unit = mid_level * mid_scale
     d_normed = d_normed_ref[...]
-    mid_grad = d_normed * unit
     d_unit = d_normed * gain_mid
     d_level = back.astype(F32) + mid_scale * (d_unit - unit * jnp.mean(d_unit * unit, axis=0, keepdims=True))
     d_bf = d_level.astype(BF16)
-    d_low = (d_level - d_bf.astype(F32)).astype(BF16)
-    both = jnp.concatenate([own, 3 - own], 1)
-    sub8 = lax.broadcasted_iota(jnp.int32, (8, 2 * local_len), 0)
-    own_hot = jnp.where(sub8 == both, 1.0, 0.0).astype(BF16)
-    ones = jnp.ones((8, 2 * local_len), BF16)
-    m_bf = mid_grad.astype(BF16)
-    m_low = (mid_grad - m_bf.astype(F32)).astype(BF16)
-    base_part_sum = dot(own_hot, d_bf, ((1,), (1,))) + dot(own_hot, d_low, ((1,), (1,)))
-    mid_part_sum = dot(ones, m_bf, ((1,), (1,))) + dot(ones, m_low, ((1,), (1,)))
-
-    open_pair(2)
+    take_in(0, [0])
 
     grad_filter = jnp.zeros((channels, block_len), F32)
     kmer_sum = jnp.zeros((half, channels), F32)
@@ -405,42 +417,69 @@
         for j in range(n_seq):
             top = j * own_rows + i // lanes_in * piece_rows
             gf[i % 2, i // 2, j] = block[top : top + piece_rows, :]
+    f_base, s_base = sems.take(), sems.take(bits)
+    sems.start(f_base, gf.at[1 - core], rf, mate)
+    take_in(2, [0])
+    mid_grad = d_normed * unit
+    d_low = (d_level - d_bf.astype(F32)).astype(BF16)
+    both = jnp.concatenate([own, 3 - own], 1)
+    sub8 = lax.broadcasted_iota(jnp.int32, (8, 2 * local_len), 0)
+    own_hot = jnp.where(sub8 == both, 1.0, 0.0).astype(BF16)
+    ones = jnp.ones((8, 2 * local_len), BF16)
+    m_bf = mid_grad.astype(BF16)
+    m_low = (mid_grad - m_bf.astype(F32)).astype(BF16)
+    base_part_sum = dot(own_hot, d_bf, ((1,), (1,))) + dot(own_hot, d_low, ((1,), (1,)))
+    mid_part_sum = dot(ones, m_bf, ((1,), (1,))) + dot(ones, m_low, ((1,), (1,)))
     rows_half = sm.shape[1]
     joined = jnp.concatenate([kmer_sum, base_part_sum, mid_part_sum], 0)
     sm[0] = joined[:rows_half]
     sm[1] = joined[rows_half:]
-    f_base, s_base = sems.take(), sems.take(bits)
-    sems.start(f_base, gf.at[1 - core], rf, mate)
     sems.start(s_base, sm.at[1 - core], s_rec.at[0], mate)
-
-    middle(0)
-    across(0)
-    across(1)
 
     sems.arrived(f_base, rf, here)
     for q in range(pairs):
         mf[q] = (gf[core, q].astype(F32) + rf[q].astype(F32)).astype(BF16)
-    for which in range(n_first):
-        for c in (4, 5):
-            streams[c].send_first(dp, sq, which)
-    for b in range(bits):
+    launch(2 * N_TILES)
+    last_t = N_TILES - 1
+    swap(last_t, keep[0], keep[1], keep[2])
+
+    def small_step(b):
         sems.arrived(s_base + b, s_rec.at[b], here)
         s_acc[b] = (sm[core] if b == 0 else s_acc[b - 1]) + s_rec[b]
         if b + 1 < bits:
             sems.start(s_base + b + 1, s_acc.at[b], s_rec.at[b + 1], (flip(dp, 2 << b), sq))
+
+    small_step(0)
+    take_in(0, range(1, bits - 1))
+    across(0)
+    open_chunk(last_t)
+    take_in(2, range(1, bits - 1))
+    across(1)
+    combined = (level_ref[...] + down_ref[...]).astype(BF16)
+    out[:channels, :] = combined[:, :local_len]
+    out[channels:, :] = dot(turn, combined[:, local_len:], ((1,), (0,))).astype(BF16)
+    take_in(2 * N_TILES, [0])
+    for b in range(1, bits):
+        small_step(b)
+    take_in(2 * N_TILES, range(1, bits - 1))
+    zf_base = sems.take(n_seq - 1)
+    for k in range(1, n_seq):
+        sems.start(zf_base + k - 1, mf.at[me_q, flip(sq, k)], yf.at[k - 1], (dp, flip(sq, k)))
     zs_base = sems.take(n_seq - 1)
     zs_rec[sq] = s_acc[bits - 1]
     for k in range(1, n_seq):
         sems.start(zs_base + k - 1, s_acc.at[bits - 1], zs_rec.at[sq], (dp, flip(sq, k)))
-
-    middle(4)
-    zf_base = sems.take(n_seq - 1)
-    for k in range(1, n_seq):
-        sems.start(zf_base + k - 1, mf.at[me_q, flip(sq, k)], yf.at[k - 1], (dp, flip(sq, k)))
-    middle(2)
-    across(2)
-    across(3)
-
+    take_in(2 * last_t, range(bits - 1))
+    across(last_t)
+
+    total = mf[me_q, sq].astype(F32)
+    for k in range(1, n_seq):
+        sems.arrived(zf_base + k - 1, yf.at[k - 1], here)
+        total = total + yf[k - 1].astype(F32)
+    filt_out[dp] = total.astype(BF16)
+    ring_base = sems.take(n_dp - 1)
+    for mask in range(1, n_dp):
+        sems.start(ring_base + mask - 1, filt_out.at[dp], filt_out.at[dp], (flip(dp, mask), sq))
     for k in range(1, n_seq):
         sems.arrived(zs_base + k - 1, zs_rec.at[flip(sq, k)], here)
     total = zs_rec[0]
@@ -449,23 +488,14 @@
     small_out[core] = total
     back_base = sems.take()
     sems.start(back_base, small_out.at[core], small_out.at[core], mate)
-
-    total = mf[me_q, sq].astype(F32)
-    for k in range(1, n_seq):
-        sems.arrived(zf_base + k - 1, yf.at[k - 1], here)
-        total = total + yf[k - 1].astype(F32)
-    filt_out[dp] = total.astype(BF16)
-    ring_base = sems.take(n_dp - 1)
-    for mask in range(1, n_dp):
-        sems.start(ring_base + mask - 1, filt_out.at[dp], filt_out.at[dp], (flip(dp, mask), sq))
-    at = 0
-    for c in range(4):
-        total = z_out[c][sq].astype(F32)
+    for t in range(N_TILES):
+        total = z_out[t, sq].astype(F32)
         for k in range(1, n_seq):
-            sems.arrived(zm_base + c * (n_seq - 1) + k - 1, z_in[c].at[k - 1], here)
-            total = total + z_in[c][k - 1].astype(F32)
-        mlp_out[at : at + sizes[c], :] = total
-        at += sizes[c]
+            sems.arrived(zm_base + t * (n_seq - 1) + k - 1, z_in.at[t, k - 1], here)
+            total = total + z_in[t, k - 1].astype(F32)
+        total = unpack(total, chunk, cols)
+        for j in range(part // span):
+            mlp_out[j * span + t * group : j * span + (t + 1) * group, :] = total[j * group : (j + 1) * group, :]
     sems.arrived(back_base, small_out.at[1 - core], here)
     for mask in range(1, n_dp):
         sems.arrived(ring_base + mask - 1, filt_out.at[flip(dp, mask)], here)
@@ -516,10 +546,14 @@
     n_taps = taps.shape[0]
     pairs, bits = n_dp // 2, n_dp.bit_length() - 1
     part = mlp_weights.shape[0] // n_dp
-    sizes = chunk_rows(part)
+    hidden = mlp_weights.shape[0] // 3
+    chunk = part // N_TILES
+    upper = color_rows(chunk)
     cols = channels // n_seq
     piece = (own_rows // (n_dp // lanes_in), wide)
     rows_half = (4 * n_taps + 16) // 2
+    main = pack_rows(chunk, cols)
+    packed = (main, 128) if main else (chunk, cols)
     orders = [[*range(bits - 1)], [*range(1, bits - 1)] + [0] if bits > 1 else []]
     two = 2 * local_len
 
@@ -527,10 +561,13 @@
         return pltpu.VMEM(shape, dtype)
 
     stage_bufs = []
-    for c in range(6):
+    for c in range(2 * N_TILES + 2):
         order = orders[c % 2]
         split = n_seq // 2
-        tail = (sizes[c], channels) if c < 4 else ((split if c == 4 else n_seq - split,) + piece)
+        if c < 2 * N_TILES:
+            tail = (chunk - upper if c % 2 else upper, channels)
+        else:
+            tail = (n_seq - split if c % 2 else split,) + piece
         for s in range(bits - 1):
             stage_bufs.append(v((len(stage_masks(order, s, pairs)),) + tail))
     n_sems = sem_count(n_dp, n_seq, lanes_in)
@@ -559,17 +596,19 @@
             v((channels, two)),
             v((channels, two), F32),
             v((channels, two), F32),
-            v((mlp_weights.shape[0] // 3, two), F32),
+            v((N_TILES, hidden // N_TILES, two), F32),
         ]
-        + [v((2, pairs, size, channels)) for size in sizes]
-        + [v((pairs, size, channels)) for size in sizes]
-        + [v((pairs, size, channels)) for size in sizes]
-        + [v((2, pairs, n_seq) + piece), v((pairs, n_seq) + piece), v((pairs, n_seq) + piece)]
-        + [v((n_seq, size, cols)) for size in sizes]
-        + [v((n_seq - 1, size, cols)) for size in sizes]
         + [
+            v((N_TILES, 2, pairs, chunk, channels)),
+            v((N_TILES, pairs, chunk, channels)),
+            v((N_TILES, pairs, chunk, channels)),
+            v((N_TILES, n_seq) + packed),
+            v((N_TILES, n_seq - 1) + packed),
+            v((3, hidden // N_TILES, two)),
+            v((2, pairs, n_seq) + piece),
+            v((pairs, n_seq) + piece),
+            v((pairs, n_seq) + piece),
             v((n_seq - 1,) + piece),
-            v(piece),
             v((2, rows_half, channels), F32),
             v((bits, rows_half, channels), F32),
             v((bits, rows_half, channels), F32),

time: 54.3 us -> 48 us (0.88)
  Pallas kernels: 53.5 us -> 47.1 us
    pallas_call x1, Pallas kernels: 51.3 us -> 44.9 us  [on_device(): pl.pallas_call(lambda *refs: mega_kernel(n_dp, n_seq, lanes_in, *refs), o...]
where the time goes in v3:
time: 48 us; the launch traced here: 47.8 us
  Pallas kernels  47.1 us (98%)
  between operations  0.64 us (1%)
    pallas_call x1, Pallas kernels, on_device(): pl.pallas_call(lambda *refs: mega_kernel(n_dp, n_seq, lanes_in, *refs), o...  44.9 us
    pallas_call x1, Pallas kernels, on_device(): pl.pallas_call(lambda *refs: finish_kernel(n_taps, *refs), out_shape=(jax...  2.24 us

profile of v3, /device:TPU:0, one launch (start us, length us, event | category | flops | bytes accessed | tf_op | source)
XLA Modules:
  0.0 47.8 jit_solution(638103681384641888)
XLA Ops:
  0.6 44.9 %mega.1 = (bf16[768,256]{1,0:T(8,128)(2,1)}, f32[288,96]{1,0:T(8,128)}, bf16[8,96,128]{2,1,0:T(8,128)(2,1)}, f32[2,16,384]{2,1,0:T(8,128)}) custom-call(s32[1,256]{1,0:T(1,128)} %refs_0_.1, f32[4,384]{1,0:T(4,128)} %refs_4_.1, f32[384]{0:T(512)} %refs_5_.3, f32[384]{0:T(512)} %refs_3_.1, f32[4,384]{1,0:T(4,128)} %bitcast.5, f32[96,1024]{1,0:T(8,128)} %refs_5_.2, ...), custom_call_target="tpu_custom_call" | custom-call | tf_op jit(solution)/shard_map/mega/pallas_call | solution.py:577
  45.5 2.2 %finish.1 = (bf16[768,256]{1,0:T(8,128)(2,1)}, f32[4,384]{1,0:T(4,128)}, f32[384]{0:T(512)}, f32[4,384]{1,0:T(4,128)}, f32[96,1024]{1,0:T(8,128)}, /*index=5*/f32[384]{0:T(512)}, f32[288,96]{1,0:T(8,128)}) custom-call(bf16[768,256]{1,0:T(8,128)(2,1)} %get-tuple-element.18.refs_0_, f32[288,96]{1,0:T(8,128)} %get-tuple-element.19.refs_1_, ...), custom_call_target="tpu_custom_call" | custom-call | tf_op jit(solution)/shard_map/finish/pallas_call | solution.py:628

commit v4 on v3

--- a/solution.py
+++ b/solution.py
@@ -146,8 +146,9 @@
 
 def mega_kernel(
     n_dp, n_seq, lanes_in,
-    ids, emb, gin, gmid, taps_in, shard, table_h, mlp_h, cot_h,
-    out, mlp_out, filt_out, small_out,
+    ids_h, emb_h, gin_h, gmid_h, taps_h, shard_h, table_h, mlp_h, cot_h,
+    out_h, mlp_out_h, filt_out_h, small_out_h,
+    ids, emb, gin, gmid, taps_in, shard, out, mlp_out, filt_out, small_out,
     table, mlp, cot, gath, all_ids, full, spec_ref, level_ref, normed_ref, d_normed_ref, down_ref, d_act_ref,
     grads, recs0, sums, z_out, z_in, keep, gf, rf, mf, yf,
     sm, s_rec, s_acc, zs_rec,
@@ -176,20 +177,23 @@
     wide = block_len // lanes_in
     lane_at = lax.rem(dp, lanes_in)
 
-    loads = [
-        pltpu.make_async_copy(table_h, table, load_sem.at[0]),
-        pltpu.make_async_copy(cot_h, cot, load_sem.at[1]),
-        pltpu.make_async_copy(mlp_h, mlp, load_sem.at[2]),
-    ]
-    for load in loads:
+    moves = (
+        (shard_h, shard), (ids_h, ids), (emb_h, emb), (gin_h, gin), (gmid_h, gmid), (taps_h, taps_in),
+        (cot_h, cot), (table_h, table), (mlp_h, mlp),
+        (out, out_h), (mlp_out, mlp_out_h), (filt_out, filt_out_h), (small_out, small_out_h),
+    )
+    loads = [pltpu.make_async_copy(a, b, load_sem.at[n]) for n, (a, b) in enumerate(moves)]
+    for load in loads[:9]:
         load.start()
     barrier = pltpu.get_barrier_semaphore()
     for mask in range(1, n_dp):
         pl.semaphore_signal(barrier, inc=1, device_id=(flip(dp, mask), sq), device_id_type=MESH)
     for mask in range(1, n_seq):
         pl.semaphore_signal(barrier, inc=1, device_id=(dp, flip(sq, mask)), device_id_type=MESH)
+    loads[0].wait()
     for p in range(lanes_in):
         gath[p, sq] = shard[:, p * wide : (p + 1) * wide].astype(BF16)
+    loads[1].wait()
     all_ids[sq] = ids[...]
     pl.semaphore_wait(barrier, n_dp + n_seq - 2)
 
@@ -201,6 +205,8 @@
         sems.start(z_base + k - 1, gath.at[lane_at, sq], gath.at[lane_at, sq], to)
 
     pad = 128 - 6 - n_taps
+    for load in loads[2:6]:
+        load.wait()
     rows_all = jnp.concatenate(
         [
             emb[...],
@@ -231,7 +237,7 @@
         1.0,
         0.0,
     ).astype(BF16)
-    loads[1].wait()
+    loads[6].wait()
     turned = dot(turn, cot[channels:, :], ((1,), (0,))).astype(BF16)
     back = jnp.concatenate([cot[:channels, :], turned], 1)
 
@@ -274,11 +280,11 @@
             want = sub % 4 if s == 0 else 3 - sub % 4
             tiles.append(jnp.where(picked == want, 1.0, 0.0))
     hot = jnp.concatenate(tiles, 0).astype(BF16)
-    loads[0].wait()
+    loads[7].wait()
     hot_spec = dot(hot, table[...], ((1,), (0,))).astype(BF16)
     for s in range(2):
         spec_ref[s] = dot(kmer, hot_spec[s * half : (s + 1) * half], ((1,), (0,))).astype(BF16)
-    loads[2].wait()
+    loads[8].wait()
     for t in range(N_TILES):
         w_down = jnp.concatenate(
             [mlp[2 * hidden + h * span + t * group : 2 * hidden + h * span + (t + 1) * group, :] for h in range(hidden // span)], 0
@@ -393,55 +399,15 @@
         down_ref[...] = down if t == 0 else down_ref[...] + down
         d_part = dot(w_gate, d_gate, ((0,), (0,))) + dot(w_up, d_up, ((0,), (0,)))
         d_normed_ref[...] = d_part if t == 0 else d_normed_ref[...] + d_part
-
-    mid_level = level_ref[...]
-    unit = mid_level * mid_scale
-    d_normed = d_normed_ref[...]
-    d_unit = d_normed * gain_mid
-    d_level = back.astype(F32) + mid_scale * (d_unit - unit * jnp.mean(d_unit * unit, axis=0, keepdims=True))
-    d_bf = d_level.astype(BF16)
-    take_in(0, [0])
-
-    grad_filter = jnp.zeros((channels, block_len), F32)
-    kmer_sum = jnp.zeros((half, channels), F32)
-    for s in range(2):
-        d_scaled = dot(d_bf[:, s * local_len : (s + 1) * local_len], q_own, ((1,), (0,)))
-        grad_filter = grad_filter + d_scaled * spec_ref[s].astype(F32)
-        d_spec = (full[...] * d_scaled).astype(BF16)
-        kmer_sum = kmer_sum + dot(hot_spec[s * half : (s + 1) * half], d_spec, ((1,), (1,)))
-    grad_filter = grad_filter.astype(BF16)
+    f_base, s_base = sems.take(), sems.take(bits)
+    zf_base, zs_base = sems.take(n_seq - 1), sems.take(n_seq - 1)
+    ring_base, back_base = sems.take(n_dp - 1), sems.take()
+    rows_half = sm.shape[1]
     groups = n_dp // lanes_in
     piece_rows = own_rows // groups
-    for i in range(n_dp):
-        block = grad_filter[:, i % lanes_in * wide : (i % lanes_in + 1) * wide]
-        for j in range(n_seq):
-            top = j * own_rows + i // lanes_in * piece_rows
-            gf[i % 2, i // 2, j] = block[top : top + piece_rows, :]
-    f_base, s_base = sems.take(), sems.take(bits)
-    sems.start(f_base, gf.at[1 - core], rf, mate)
-    take_in(2, [0])
-    mid_grad = d_normed * unit
-    d_low = (d_level - d_bf.astype(F32)).astype(BF16)
-    both = jnp.concatenate([own, 3 - own], 1)
-    sub8 = lax.broadcasted_iota(jnp.int32, (8, 2 * local_len), 0)
-    own_hot = jnp.where(sub8 == both, 1.0, 0.0).astype(BF16)
-    ones = jnp.ones((8, 2 * local_len), BF16)
-    m_bf = mid_grad.astype(BF16)
-    m_low = (mid_grad - m_bf.astype(F32)).astype(BF16)
-    base_part_sum = dot(own_hot, d_bf, ((1,), (1,))) + dot(own_hot, d_low, ((1,), (1,)))
-    mid_part_sum = dot(ones, m_bf, ((1,), (1,))) + dot(ones, m_low, ((1,), (1,)))
-    rows_half = sm.shape[1]
-    joined = jnp.concatenate([kmer_sum, base_part_sum, mid_part_sum], 0)
-    sm[0] = joined[:rows_half]
-    sm[1] = joined[rows_half:]
-    sems.start(s_base, sm.at[1 - core], s_rec.at[0], mate)
-
-    sems.arrived(f_base, rf, here)
-    for q in range(pairs):
-        mf[q] = (gf[core, q].astype(F32) + rf[q].astype(F32)).astype(BF16)
-    launch(2 * N_TILES)
     last_t = N_TILES - 1
-    swap(last_t, keep[0], keep[1], keep[2])
+    f_at = 2 * N_TILES
+    rest_of = range(1, bits - 1)
 
     def small_step(b):
         sems.arrived(s_base + b, s_rec.at[b], here)
@@ -449,46 +415,85 @@
         if b + 1 < bits:
             sems.start(s_base + b + 1, s_acc.at[b], s_rec.at[b + 1], (flip(dp, 2 << b), sq))
 
-    small_step(0)
-    take_in(0, range(1, bits - 1))
-    across(0)
-    open_chunk(last_t)
-    take_in(2, range(1, bits - 1))
-    across(1)
-    combined = (level_ref[...] + down_ref[...]).astype(BF16)
-    out[:channels, :] = combined[:, :local_len]
-    out[channels:, :] = dot(turn, combined[:, local_len:], ((1,), (0,))).astype(BF16)
-    take_in(2 * N_TILES, [0])
-    for b in range(1, bits):
-        small_step(b)
-    take_in(2 * N_TILES, range(1, bits - 1))
-    zf_base = sems.take(n_seq - 1)
-    for k in range(1, n_seq):
-        sems.start(zf_base + k - 1, mf.at[me_q, flip(sq, k)], yf.at[k - 1], (dp, flip(sq, k)))
-    zs_base = sems.take(n_seq - 1)
-    zs_rec[sq] = s_acc[bits - 1]
-    for k in range(1, n_seq):
-        sems.start(zs_base + k - 1, s_acc.at[bits - 1], zs_rec.at[sq], (dp, flip(sq, k)))
-    take_in(2 * last_t, range(bits - 1))
-    across(last_t)
-
-    total = mf[me_q, sq].astype(F32)
-    for k in range(1, n_seq):
-        sems.arrived(zf_base + k - 1, yf.at[k - 1], here)
-        total = total + yf[k - 1].astype(F32)
-    filt_out[dp] = total.astype(BF16)
-    ring_base = sems.take(n_dp - 1)
-    for mask in range(1, n_dp):
-        sems.start(ring_base + mask - 1, filt_out.at[dp], filt_out.at[dp], (flip(dp, mask), sq))
-    for k in range(1, n_seq):
-        sems.arrived(zs_base + k - 1, zs_rec.at[flip(sq, k)], here)
-    total = zs_rec[0]
-    for j in range(1, n_seq):
-        total = total + zs_rec[j]
-    small_out[core] = total
-    back_base = sems.take()
-    sems.start(back_base, small_out.at[core], small_out.at[core], mate)
-    for t in range(N_TILES):
+    def level_grad():
+        unit = level_ref[...] * mid_scale
+        d_normed = d_normed_ref[...]
+        d_unit = d_normed * gain_mid
+        return back.astype(F32) + mid_scale * (d_unit - unit * jnp.mean(d_unit * unit, axis=0, keepdims=True))
+
+    def filter_part(d_bf):
+        grad_filter = jnp.zeros((channels, block_len), F32)
+        kmer_sum = jnp.zeros((half, channels), F32)
+        for s in range(2):
+            d_scaled = dot(d_bf[:, s * local_len : (s + 1) * local_len], q_own, ((1,), (0,)))
+            grad_filter = grad_filter + d_scaled * spec_ref[s].astype(F32)
+            d_spec = (full[...] * d_scaled).astype(BF16)
+            kmer_sum = kmer_sum + dot(hot_spec[s * half : (s + 1) * half], d_spec, ((1,), (1,)))
+        grad_filter = grad_filter.astype(BF16)
+        for i in range(n_dp):
+            block = grad_filter[:, i % lanes_in * wide : (i % lanes_in + 1) * wide]
+            for j in range(n_seq):
+                top = j * own_rows + i // lanes_in * piece_rows
+                gf[i % 2, i // 2, j] = block[top : top + piece_rows, :]
+        sems.start(f_base, gf.at[1 - core], rf, mate)
+        return kmer_sum
+
+    def small_part(d_level, d_bf, kmer_sum):
+        mid_grad = d_normed_ref[...] * (level_ref[...] * mid_scale)
+        d_low = (d_level - d_bf.astype(F32)).astype(BF16)
+        both = jnp.concatenate([own, 3 - own], 1)
+        sub8 = lax.broadcasted_iota(jnp.int32, (8, 2 * local_len), 0)
+        own_hot = jnp.where(sub8 == both, 1.0, 0.0).astype(BF16)
+        ones = jnp.ones((8, 2 * local_len), BF16)
+        m_bf = mid_grad.astype(BF16)
+        m_low = (mid_grad - m_bf.astype(F32)).astype(BF16)
+        base_part_sum = dot(own_hot, d_bf, ((1,), (1,))) + dot(own_hot, d_low, ((1,), (1,)))
+        mid_part_sum = dot(ones, m_bf, ((1,), (1,))) + dot(ones, m_low, ((1,), (1,)))
+        joined = jnp.concatenate([kmer_sum, base_part_sum, mid_part_sum], 0)
+        sm[0] = joined[:rows_half]
+        sm[1] = joined[rows_half:]
+        sems.start(s_base, sm.at[1 - core], s_rec.at[0], mate)
+
+    def open_filter():
+        sems.arrived(f_base, rf, here)
+        for q in range(pairs):
+            mf[q] = (gf[core, q].astype(F32) + rf[q].astype(F32)).astype(BF16)
+        launch(f_at)
+
+    def write_out():
+        combined = (level_ref[...] + down_ref[...]).astype(BF16)
+        out[:channels, :] = combined[:, :local_len]
+        out[channels:, :] = dot(turn, combined[:, local_len:], ((1,), (0,))).astype(BF16)
+        loads[9].start()
+
+    def filter_across():
+        for k in range(1, n_seq):
+            sems.start(zf_base + k - 1, mf.at[me_q, flip(sq, k)], yf.at[k - 1], (dp, flip(sq, k)))
+
+    def small_across():
+        zs_rec[sq] = s_acc[bits - 1]
+        for k in range(1, n_seq):
+            sems.start(zs_base + k - 1, s_acc.at[bits - 1], zs_rec.at[sq], (dp, flip(sq, k)))
+
+    def filter_ring():
+        total = mf[me_q, sq].astype(F32)
+        for k in range(1, n_seq):
+            sems.arrived(zf_base + k - 1, yf.at[k - 1], here)
+            total = total + yf[k - 1].astype(F32)
+        filt_out[dp] = total.astype(BF16)
+        for mask in range(1, n_dp):
+            sems.start(ring_base + mask - 1, filt_out.at[dp], filt_out.at[dp], (flip(dp, mask), sq))
+
+    def small_back():
+        for k in range(1, n_seq):
+            sems.arrived(zs_base + k - 1, zs_rec.at[flip(sq, k)], here)
+        total = zs_rec[0]
+        for j in range(1, n_seq):
+            total = total + zs_rec[j]
+        small_out[core] = total
+        sems.start(back_base, small_out.at[core], small_out.at[core], mate)
+
+    def finish_chunk(t):
         total = z_out[t, sq].astype(F32)
         for k in range(1, n_seq):
             sems.arrived(zm_base + t * (n_seq - 1) + k - 1, z_in.at[t, k - 1], here)
@@ -496,23 +501,74 @@
         total = unpack(total, chunk, cols)
         for j in range(part // span):
             mlp_out[j * span + t * group : j * span + (t + 1) * group, :] = total[j * group : (j + 1) * group, :]
+
+    d_level = level_grad()
+    d_bf = d_level.astype(BF16)
+    kmer_sum = filter_part(d_bf)
+    small_part(d_level, d_bf, kmer_sum)
+    take_in(0, [0])
+    open_filter()
+    swap(last_t, keep[0], keep[1], keep[2])
+    take_in(2, [0])
+    small_step(0)
+    take_in(0, rest_of)
+    across(0)
+    take_in(f_at, [0])
+    open_chunk(last_t)
+    small_step(1)
+    write_out()
+    take_in(f_at, rest_of)
+    filter_across()
+    take_in(2, rest_of)
+    across(1)
+    for b in range(2, bits):
+        small_step(b)
+    small_across()
+    take_in(2 * last_t, [0])
+    take_in(2 * last_t, rest_of)
+    across(last_t)
+    filter_ring()
+    small_back()
+    finish_chunk(0)
+    finish_chunk(1)
+    finish_chunk(last_t)
+    loads[10].start()
     sems.arrived(back_base, small_out.at[1 - core], here)
+    loads[12].start()
     for mask in range(1, n_dp):
         sems.arrived(ring_base + mask - 1, filt_out.at[flip(dp, mask)], here)
+    loads[11].start()
     sems.drain()
+    for load in loads[9:]:
+        load.wait()
 
 
 def finish_kernel(
-    n_taps, layer, mlp_sum, filt, small, embedding, gain_in, taps,
-    layer_out, grad_emb, grad_gain, grad_conv, filt_out, grad_mid, mlp_out,
+    n_taps, layer_h, mlp_sum_h, filt_h, small_h, emb_h, gain_h, taps_h,
+    layer_out_h, grad_emb_h, grad_gain_h, grad_conv_h, filt_out_h, grad_mid_h, mlp_out_h,
+    layer, mlp_sum, filt, small, embedding, gain_in, taps,
+    grad_emb, grad_gain, grad_conv, filt_out, grad_mid, sem,
 ):
-    layer_out[...] = layer[...]
-    mlp_out[...] = mlp_sum[...]
+    moves = (
+        (layer_h, layer), (filt_h, filt), (small_h, small), (emb_h, embedding), (gain_h, gain_in), (taps_h, taps),
+        (mlp_sum_h, mlp_sum), (layer, layer_out_h), (mlp_sum, mlp_out_h), (filt_out, filt_out_h),
+        (grad_emb, grad_emb_h), (grad_gain, grad_gain_h), (grad_conv, grad_conv_h), (grad_mid, grad_mid_h),
+    )
+    copies = [pltpu.make_async_copy(a, b, sem.at[n]) for n, (a, b) in enumerate(moves)]
+    for copy in copies[:7]:
+        copy.start()
+    copies[0].wait()
+    copies[7].start()
+    copies[1].wait()
     n_dp, rows, wide = filt.shape
     lanes_in = filt_out.shape[1] // wide
     for i in range(n_dp):
         top, left = i // lanes_in * rows, i % lanes_in * wide
         filt_out[top : top + rows, left : left + wide] = filt[i].astype(F32)
+    copies[9].start()
+    for copy in copies[2:7]:
+        copy.wait()
+    copies[8].start()
     channels = embedding.shape[1]
     sums = jnp.concatenate([small[0], small[1]], 0)
     emb = embedding[...]
@@ -530,6 +586,10 @@
     base_sum = sums[4 * n_taps : 4 * n_taps + 4, :]
     grad_emb[...] = base_sum + base_scale * (d_unit - unit * jnp.mean(d_unit * unit, axis=1, keepdims=True))
     grad_mid[...] = sums[4 * n_taps + 8 : 4 * n_taps + 9, :].reshape(channels)
+    for copy in copies[10:]:
+        copy.start()
+    for copy in copies[7:]:
+        copy.wait()
 
 
 def on_device(tokens, embedding, gain_in, conv_taps, long_filter, gain_mid, mlp_weights, cotangent):
@@ -582,9 +642,19 @@
             jax.ShapeDtypeStruct((n_dp,) + piece, BF16),
             jax.ShapeDtypeStruct((2, rows_half, channels), F32),
         ),
-        in_specs=[vmem] * 6 + [hbm] * 3,
-        out_specs=[vmem] * 4,
+        in_specs=[hbm] * 9,
+        out_specs=[hbm] * 4,
         scratch_shapes=[
+            v(tokens.shape, jnp.int32),
+            v(embedding.shape, F32),
+            v(gain_in.shape, F32),
+            v(gain_mid.shape, F32),
+            v(taps.shape, F32),
+            v(long_filter.shape, F32),
+            v(cot.shape),
+            v((part, cols), F32),
+            v((n_dp,) + piece),
+            v((2, rows_half, channels), F32),
             v(table.shape),
             v(mlp_weights.shape),
             v(cot.shape),
@@ -616,7 +686,7 @@
         ]
         + stage_bufs
         + [
-            pltpu.SemaphoreType.DMA((3,)),
+            pltpu.SemaphoreType.DMA((13,)),
             pltpu.SemaphoreType.DMA((n_sems,)),
             pltpu.SemaphoreType.DMA((n_sems,)),
         ],
@@ -636,8 +706,23 @@
             jax.ShapeDtypeStruct(gain_mid.shape, F32),
             jax.ShapeDtypeStruct((part, cols), F32),
         ),
-        in_specs=[vmem] * 7,
-        out_specs=[vmem] * 7,
+        in_specs=[hbm] * 7,
+        out_specs=[hbm] * 7,
+        scratch_shapes=[
+            v(cot.shape),
+            v((part, cols), F32),
+            v((n_dp,) + piece),
+            v((2, rows_half, channels), F32),
+            v(embedding.shape, F32),
+            v(gain_in.shape, F32),
+            v(taps.shape, F32),
+            v(embedding.shape, F32),
+            v(gain_in.shape, F32),
+            v(taps.shape, F32),
+            v(long_filter.shape, F32),
+            v(gain_mid.shape, F32),
+            pltpu.SemaphoreType.DMA((14,)),
+        ],
         compiler_params=pltpu.CompilerParams(vmem_limit_bytes=62 * 2**20),
         name="finish",
     )(layer, mlp_sum, filt, small, embedding, gain_in, taps)

time: 48 us -> 44.6 us (0.929)
  Pallas kernels: 47.1 us -> 43.8 us
    pallas_call x1, Pallas kernels: 44.9 us -> 41.7 us  [on_device(): pl.pallas_call(lambda *refs: mega_kernel(n_dp, n_seq, lanes_in, *refs), o...]
where the time goes in v4:
time: 44.6 us; the launch traced here: 44.4 us
  Pallas kernels  43.8 us (98%)
  between operations  0.64 us (1%)
    pallas_call x1, Pallas kernels, on_device(): pl.pallas_call(lambda *refs: mega_kernel(n_dp, n_seq, lanes_in, *refs), o...  41.7 us
    pallas_call x1, Pallas kernels, on_device(): pl.pallas_call(lambda *refs: finish_kernel(n_taps, *refs), out_shape=(jax...  2.1 us

profile of v4, /device:TPU:0, one launch (start us, length us, event | category | flops | bytes accessed | tf_op | source)
XLA Modules:
  0.0 44.4 jit_solution(2728073629647371007)
XLA Ops:
  0.6 41.7 %mega.1 = (bf16[768,256]{1,0:T(8,128)(2,1)}, f32[288,96]{1,0:T(8,128)}, bf16[8,96,128]{2,1,0:T(8,128)(2,1)}, f32[2,16,384]{2,1,0:T(8,128)}) custom-call(s32[1,256]{1,0:T(1,128)} %refs_0_.1, f32[4,384]{1,0:T(4,128)} %refs_4_.1, f32[384]{0:T(512)} %refs_5_.3, f32[384]{0:T(512)} %refs_3_.1, f32[4,384]{1,0:T(4,128)} %bitcast.5, f32[96,1024]{1,0:T(8,128)} %refs_5_.2, ...), custom_call_target="tpu_custom_call" | custom-call | tf_op jit(solution)/shard_map/mega/pallas_call | solution.py:637
  42.3 2.1 %finish.1 = (bf16[768,256]{1,0:T(8,128)(2,1)}, f32[4,384]{1,0:T(4,128)}, f32[384]{0:T(512)}, f32[4,384]{1,0:T(4,128)}, f32[96,1024]{1,0:T(8,128)}, /*index=5*/f32[384]{0:T(512)}, f32[288,96]{1,0:T(8,128)}) custom-call(bf16[768,256]{1,0:T(8,128)(2,1)} %get-tuple-element.18.refs_0_, f32[288,96]{1,0:T(8,128)} %get-tuple-element.19.refs_1_, ...), custom_call_target="tpu_custom_call" | custom-call | tf_op jit(solution)/shard_map/finish/pallas_call | solution.py:698

commit v5 on v4

--- a/solution.py
+++ b/solution.py
@@ -147,8 +147,8 @@
 def mega_kernel(
     n_dp, n_seq, lanes_in,
     ids_h, emb_h, gin_h, gmid_h, taps_h, shard_h, table_h, mlp_h, cot_h,
-    out_h, mlp_out_h, filt_out_h, small_out_h,
-    ids, emb, gin, gmid, taps_in, shard, out, mlp_out, filt_out, small_out,
+    out, mlp_out, filt_out, small_out,
+    ids, emb, gin, gmid, taps_in, shard,
     table, mlp, cot, gath, all_ids, full, spec_ref, level_ref, normed_ref, d_normed_ref, down_ref, d_act_ref,
     grads, recs0, sums, z_out, z_in, keep, gf, rf, mf, yf,
     sm, s_rec, s_acc, zs_rec,
@@ -180,10 +180,9 @@
     moves = (
         (shard_h, shard), (ids_h, ids), (emb_h, emb), (gin_h, gin), (gmid_h, gmid), (taps_h, taps_in),
         (cot_h, cot), (table_h, table), (mlp_h, mlp),
-        (out, out_h), (mlp_out, mlp_out_h), (filt_out, filt_out_h), (small_out, small_out_h),
     )
     loads = [pltpu.make_async_copy(a, b, load_sem.at[n]) for n, (a, b) in enumerate(moves)]
-    for load in loads[:9]:
+    for load in loads:
         load.start()
     barrier = pltpu.get_barrier_semaphore()
     for mask in range(1, n_dp):
@@ -464,7 +463,6 @@
         combined = (level_ref[...] + down_ref[...]).astype(BF16)
         out[:channels, :] = combined[:, :local_len]
         out[channels:, :] = dot(turn, combined[:, local_len:], ((1,), (0,))).astype(BF16)
-        loads[9].start()
 
     def filter_across():
         for k in range(1, n_seq):
@@ -532,43 +530,30 @@
     finish_chunk(0)
     finish_chunk(1)
     finish_chunk(last_t)
-    loads[10].start()
     sems.arrived(back_base, small_out.at[1 - core], here)
-    loads[12].start()
     for mask in range(1, n_dp):
         sems.arrived(ring_base + mask - 1, filt_out.at[flip(dp, mask)], here)
-    loads[11].start()
     sems.drain()
-    for load in loads[9:]:
-        load.wait()
 
 
 def finish_kernel(
-    n_taps, layer_h, mlp_sum_h, filt_h, small_h, emb_h, gain_h, taps_h,
+    n_taps, layer, mlp_sum, filt, small, embedding, gain_in, taps,
     layer_out_h, grad_emb_h, grad_gain_h, grad_conv_h, filt_out_h, grad_mid_h, mlp_out_h,
-    layer, mlp_sum, filt, small, embedding, gain_in, taps,
     grad_emb, grad_gain, grad_conv, filt_out, grad_mid, sem,
 ):
     moves = (
-        (layer_h, layer), (filt_h, filt), (small_h, small), (emb_h, embedding), (gain_h, gain_in), (taps_h, taps),
-        (mlp_sum_h, mlp_sum), (layer, layer_out_h), (mlp_sum, mlp_out_h), (filt_out, filt_out_h),
+        (layer, layer_out_h), (mlp_sum, mlp_out_h), (filt_out, filt_out_h),
         (grad_emb, grad_emb_h), (grad_gain, grad_gain_h), (grad_conv, grad_conv_h), (grad_mid, grad_mid_h),
     )
     copies = [pltpu.make_async_copy(a, b, sem.at[n]) for n, (a, b) in enumerate(moves)]
-    for copy in copies[:7]:
-        copy.start()
-    copies[0].wait()
-    copies[7].start()
-    copies[1].wait()
+    copies[0].start()
+    copies[1].start()
     n_dp, rows, wide = filt.shape
     lanes_in = filt_out.shape[1] // wide
     for i in range(n_dp):
         top, left = i // lanes_in * rows, i % lanes_in * wide
         filt_out[top : top + rows, left : left + wide] = filt[i].astype(F32)
-    copies[9].start()
-    for copy in copies[2:7]:
-        copy.wait()
-    copies[8].start()
+    copies[2].start()
     channels = embedding.shape[1]
     sums = jnp.concatenate([small[0], small[1]], 0)
     emb = embedding[...]
@@ -586,9 +571,9 @@
     base_sum = sums[4 * n_taps : 4 * n_taps + 4, :]
     grad_emb[...] = base_sum + base_scale * (d_unit - unit * jnp.mean(d_unit * unit, axis=1, keepdims=True))
     grad_mid[...] = sums[4 * n_taps + 8 : 4 * n_taps + 9, :].reshape(channels)
-    for copy in copies[10:]:
+    for copy in copies[3:]:
         copy.start()
-    for copy in copies[7:]:
+    for copy in copies:
         copy.wait()
 
 
@@ -634,6 +619,8 @@
     vmem = pl.BlockSpec(memory_space=pltpu.VMEM)
     hbm = pl.BlockSpec(memory_space=pltpu.HBM)
     cot = cotangent[0]
+    operands = [tokens, embedding, gain_in, gain_mid, taps, long_filter, table, mlp_weights, cot]
+    operands = [pltpu.with_memory_space_constraint(x, pltpu.HBM) for x in operands]
     layer, mlp_sum, filt, small = pl.pallas_call(
         lambda *refs: mega_kernel(n_dp, n_seq, lanes_in, *refs),
         out_shape=(
@@ -643,7 +630,7 @@
             jax.ShapeDtypeStruct((2, rows_half, channels), F32),
         ),
         in_specs=[hbm] * 9,
-        out_specs=[hbm] * 4,
+        out_specs=[vmem] * 4,
         scratch_shapes=[
             v(tokens.shape, jnp.int32),
             v(embedding.shape, F32),
@@ -651,10 +638,6 @@
             v(gain_mid.shape, F32),
             v(taps.shape, F32),
             v(long_filter.shape, F32),
-            v(cot.shape),
-            v((part, cols), F32),
-            v((n_dp,) + piece),
-            v((2, rows_half, channels), F32),
             v(table.shape),
             v(mlp_weights.shape),
             v(cot.shape),
@@ -686,15 +669,15 @@
         ]
         + stage_bufs
         + [
-            pltpu.SemaphoreType.DMA((13,)),
+            pltpu.SemaphoreType.DMA((9,)),
             pltpu.SemaphoreType.DMA((n_sems,)),
             pltpu.SemaphoreType.DMA((n_sems,)),
         ],
         compiler_params=pltpu.CompilerParams(
-            collective_id=0, has_side_effects=True, vmem_limit_bytes=62 * 2**20
+            collective_id=0, has_side_effects=True, vmem_limit_bytes=34 * 2**20
         ),
         name="mega",
-    )(tokens, embedding, gain_in, gain_mid, taps, long_filter, table, mlp_weights, cot)
+    )(*operands)
     layer_out, grad_emb, grad_gain, grad_conv, grad_filter, grad_mid, grad_mlp = pl.pallas_call(
         lambda *refs: finish_kernel(n_taps, *refs),
         out_shape=(
@@ -706,24 +689,17 @@
             jax.ShapeDtypeStruct(gain_mid.shape, F32),
             jax.ShapeDtypeStruct((part, cols), F32),
         ),
-        in_specs=[hbm] * 7,
+        in_specs=[vmem] * 7,
         out_specs=[hbm] * 7,
         scratch_shapes=[
-            v(cot.shape),
-            v((part, cols), F32),
-            v((n_dp,) + piece),
-            v((2, rows_half, channels), F32),
-            v(embedding.shape, F32),
-            v(gain_in.shape, F32),
-            v(taps.shape, F32),
             v(embedding.shape, F32),
             v(gain_in.shape, F32),
             v(taps.shape, F32),
             v(long_filter.shape, F32),
             v(gain_mid.shape, F32),
-            pltpu.SemaphoreType.DMA((14,)),
+            pltpu.SemaphoreType.DMA((7,)),
         ],
-        compiler_params=pltpu.CompilerParams(vmem_limit_bytes=62 * 2**20),
+        compiler_params=pltpu.CompilerParams(vmem_limit_bytes=8 * 2**20),
         name="finish",
     )(layer, mlp_sum, filt, small, embedding, gain_in, taps)
     return layer_out[None], grad_emb, grad_gain, grad_conv.T, grad_filter, grad_mid, grad_mlp

time: 44.6 us -> 43 us (0.964)
  Pallas kernels: 43.8 us -> 42.1 us
    pallas_call x1, Pallas kernels: 2.1 us -> 1 us  [on_device(): pl.pallas_call(lambda *refs: finish_kernel(n_taps, *refs), out_shape=(jax...]
    pallas_call x1, Pallas kernels: 41.7 us -> 41.1 us  [on_device(): pl.pallas_call(lambda *refs: mega_kernel(n_dp, n_seq, lanes_in, *refs), o...]
where the time goes in v5:
time: 43 us; the launch traced here: 42.8 us
  Pallas kernels  42.1 us (98%)
  between operations  0.69 us (2%)
    pallas_call x1, Pallas kernels, on_device(): pl.pallas_call(lambda *refs: mega_kernel(n_dp, n_seq, lanes_in, *refs), o...  41.1 us
    pallas_call x1, Pallas kernels, on_device(): pl.pallas_call(lambda *refs: finish_kernel(n_taps, *refs), out_shape=(jax...  1 us

profile of v5, /device:TPU:0, one launch (start us, length us, event | category | flops | bytes accessed | tf_op | source)
XLA Modules:
  0.0 42.8 jit_solution(16458018796520397610)
XLA Ops:
  0.6 0.0 copy-start
  0.6 0.0 copy-start.1
  0.7 0.0 copy-start.2
  0.7 41.1 %mega.1 = (bf16[768,256]{1,0:T(8,128)(2,1)S(1)}, f32[288,96]{1,0:T(8,128)S(1)}, bf16[8,96,128]{2,1,0:T(8,128)(2,1)S(1)}, f32[2,16,384]{2,1,0:T(8,128)S(1)}) custom-call(s32[1,256]{1,0:T(1,128)} %refs_0_.1, f32[4,384]{1,0:T(4,128)} %refs_4_.1, f32[384]{0:T(512)} %refs_5_.3, f32[384]{0:T(512)} %refs_3_.1, f32[4,384]{1,0:T(4,128)} %bitcast.4, ...), custom_call_target="tpu_custom_call" | custom-call | tf_op jit(solution)/shard_map/mega/pallas_call | solution.py:624
  41.8 0.0 copy-done
  41.8 0.0 copy-done.1
  41.8 0.0 copy-done.2
  41.8 1.0 %finish.1 = (bf16[768,256]{1,0:T(8,128)(2,1)}, f32[4,384]{1,0:T(4,128)}, f32[384]{0:T(512)}, f32[4,384]{1,0:T(4,128)}, f32[96,1024]{1,0:T(8,128)}, /*index=5*/f32[384]{0:T(512)}, f32[288,96]{1,0:T(8,128)}) custom-call(bf16[768,256]{1,0:T(8,128)(2,1)S(1)} %get-tuple-element.18.refs_0_, f32[288,96]{1,0:T(8,128)S(1)} %get-tuple-element.19.refs_1_, ...), custom_call_target="tpu_custom_call" | custom-call | tf_op jit(solution)/shard_map/finish/pallas_call | solution.py:681
Async XLA Ops:
  0.6 41.2 %copy-start = (f32[4,384]{1,0:T(4,128)S(1)}, f32[4,384]{1,0:T(4,128)}, u32[]{:S(2)}) copy-start(f32[4,384]{1,0:T(4,128)} %refs_4_.1) | copy-start | bytes 18436
  0.6 41.2 %copy-start.1 = (f32[384,4]{0,1:T(4,128)S(1)}, f32[384,4]{0,1:T(4,128)}, u32[]{:S(2)}) copy-start(f32[384,4]{0,1:T(4,128)} %param.12) | copy-start | bytes 18436
  0.7 41.2 %copy-start.2 = (f32[384]{0:T(512)S(1)}, f32[384]{0:T(512)}, u32[]{:S(2)}) copy-start(f32[384]{0:T(512)} %refs_5_.3) | copy-start | bytes 4612
